TPU v7x, 512 devices: a whole 4x4x16 slice. The times are simulated.
512 devices in a mesh: ctx: 32 (over z, y_lo), head: 16 (over y_hi, x, core).
Axes of the slice: x: 4, y: 4 (y_hi: 2, y_lo: 2; y = y_hi * 2 + y_lo), z: 16, core: 2. Of those that a mesh axis runs over, the one named last changes fastest.
Arguments:
- query: bfloat16 [65536, 1024], P(('ctx', 'head')), may hold values from -7 to 7
- key: bfloat16 [65536, 1024], P(('ctx', 'head')), may hold values from -7 to 7
- value: bfloat16 [65536, 1024], P(('ctx', 'head')), may hold values from -6 to 6
- grad_out: bfloat16 [65536, 1024], P(('ctx', 'head')), may hold values from -6 to 6
- neighbour: int32 [512, 8], replicated, may hold values from 0 to 511, as said below
- counts: int32 [512], replicated, may hold values from 1 to 8, as said below
Outputs:
- attn_out: bfloat16 [65536, 1024], P(('ctx', 'head'))
- grad_query: bfloat16 [65536, 1024], P(('ctx', 'head'))
- grad_key: bfloat16 [65536, 1024], P(('ctx', 'head'))
- grad_value: bfloat16 [65536, 1024], P(('ctx', 'head'))
Inputs may be any that keep to these rules, and one draw needn't show every extreme that they name: `neighbour`: row b lists key blocks for query block b: its first entry is b itself, and every entry lies within 32 blocks of b in the periodic block order; some row has an entry exactly 32 blocks ahead, and some row one exactly that far behind. Query block b uses the first counts[b] slots of its row; some block uses all 8 slots and some only one.
All inputs are finite; a program needn't handle non-finite values.
Results may differ from a plain program's by a relative error of at most 0.0083.
Values may be sent and summed in bfloat16 or wider, within the bound.
No kernel may reach another device: no remote copies, remote signals or barrier semaphores. Data moves between devices by JAX's collectives and lax.ppermute only.
A program may use at most 64 MiB of HBM per device.

v0:
```python
import math

import jax
import jax.numpy as jnp
from jax import lax
from jax.sharding import PartitionSpec as P

H = 16
E = 64
BLK = 128
NNB = 8
REACH = 2


def passed_along(value, axis, steps):
    count = lax.axis_size(axis)
    pairs = [(source, (source + steps) % count) for source in range(count)]
    return lax.ppermute(value, axis, pairs)


def group_rows(blocks_shard, block_len):
    limit = max(512 // block_len, 1)
    best = 1
    for candidate in range(1, blocks_shard + 1):
        if blocks_shard % candidate == 0 and candidate <= limit:
            best = candidate
    return best


def on_device(query, key, value, grad_out, neighbour, counts):
    tok_rows = query.shape[0]
    groups = lax.axis_size("head")
    per_dev = H // groups
    head_cols = per_dev * E
    moved = (
        lax.all_to_all(
            query.reshape(tok_rows, groups, head_cols),
            "head",
            split_axis=1,
            concat_axis=0,
            tiled=True,
        ),
        lax.all_to_all(
            key.reshape(tok_rows, groups, head_cols),
            "head",
            split_axis=1,
            concat_axis=0,
            tiled=True,
        ),
        lax.all_to_all(
            value.reshape(tok_rows, groups, head_cols),
            "head",
            split_axis=1,
            concat_axis=0,
            tiled=True,
        ),
        lax.all_to_all(
            grad_out.reshape(tok_rows, groups, head_cols),
            "head",
            split_axis=1,
            concat_axis=0,
            tiled=True,
        ),
    )
    shard_rows = groups * tok_rows
    query_s = moved[0].reshape(shard_rows, head_cols)
    key_s = moved[1].reshape(shard_rows, head_cols)
    value_s = moved[2].reshape(shard_rows, head_cols)
    grad_s = moved[3].reshape(shard_rows, head_cols)
    paired = jnp.concatenate([key_s, value_s], axis=1)
    cycle_len = lax.axis_size("ctx")
    position = lax.axis_index("ctx")
    blocks_shard = shard_rows // BLK
    all_blocks = blocks_shard * cycle_len
    fetched = {}
    offsets_all = list(range(1, REACH + 1)) + [-offset for offset in range(1, REACH + 1)]
    for offset in offsets_all:
        fetched[offset] = passed_along(paired, "ctx", offset)
    ordered = (
        [fetched[REACH - place] for place in range(REACH)]
        + [paired]
        + [fetched[-(place + 1)] for place in range(REACH)]
    )
    span_shards = 2 * REACH + 1
    window = jnp.concatenate(ordered, axis=0).reshape(
        span_shards * blocks_shard, BLK, 2 * head_cols
    )
    rows_nbr = lax.dynamic_slice_in_dim(neighbour, position * blocks_shard, blocks_shard, 0)
    local_idx = jnp.mod(rows_nbr - (position - REACH) * blocks_shard, all_blocks)
    used = lax.dynamic_slice_in_dim(counts, position * blocks_shard, blocks_shard, 0)
    per_group = group_rows(blocks_shard, BLK)
    turns = blocks_shard // per_group
    scale_factor = 1.0 / math.sqrt(E)
    query_g = query_s.reshape(turns, per_group, BLK, per_dev, E)
    grad_g = grad_s.reshape(turns, per_group, BLK, per_dev, E)
    index_g = local_idx.reshape(turns, per_group, NNB)
    used_g = used.reshape(turns, per_group)

    def one_group(totals, inputs):
        queries, cotangent, chosen, used_now = inputs
        selected = window[chosen]
        keys_sel = selected[..., :head_cols].reshape(per_group, NNB, BLK, per_dev, E)
        values_sel = selected[..., head_cols:].reshape(per_group, NNB, BLK, per_dev, E)
        usable = jnp.arange(NNB)[None, :] < used_now[:, None]
        allowed = usable[:, None, None, :, None]
        scores = (
            jnp.einsum("rihe,rjthe->rhijt", queries, keys_sel, preferred_element_type=jnp.float32)
            * scale_factor
        )
        masked = jnp.where(allowed, scores, -1e30)
        highest = jnp.max(masked, axis=(3, 4), keepdims=True)
        raised = jnp.where(allowed, jnp.exp(masked - highest), 0.0)
        total = jnp.sum(raised, axis=(3, 4), keepdims=True)
        probability = raised / total
        weights = probability.astype(jnp.bfloat16)
        out_rows = jnp.einsum(
            "rhijt,rjthe->rihe", weights, values_sel, preferred_element_type=jnp.float32
        ).astype(jnp.bfloat16)
        dprob = jnp.einsum(
            "rihe,rjthe->rhijt", cotangent, values_sel, preferred_element_type=jnp.float32
        )
        row_delta = jnp.sum(probability * dprob, axis=(3, 4), keepdims=True)
        dscore = (probability * (dprob - row_delta) * scale_factor).astype(jnp.bfloat16)
        dquery = jnp.einsum(
            "rhijt,rjthe->rihe", dscore, keys_sel, preferred_element_type=jnp.float32
        ).astype(jnp.bfloat16)
        dkey_part = jnp.einsum(
            "rhijt,rihe->rjthe", dscore, queries, preferred_element_type=jnp.float32
        )
        dvalue_part = jnp.einsum(
            "rhijt,rihe->rjthe", weights, cotangent, preferred_element_type=jnp.float32
        )
        joined = jnp.concatenate(
            [
                dkey_part.reshape(per_group * NNB, BLK, head_cols),
                dvalue_part.reshape(per_group * NNB, BLK, head_cols),
            ],
            axis=-1,
        )
        totals = totals.at[chosen.reshape(-1)].add(joined)
        return (totals, (out_rows, dquery))

    start_grads = jnp.zeros((span_shards * blocks_shard, BLK, 2 * head_cols), jnp.float32)
    grads_window, results = lax.scan(one_group, start_grads, (query_g, grad_g, index_g, used_g))
    grads_window = grads_window.reshape(span_shards, shard_rows, 2 * head_cols)
    combined = grads_window[REACH]
    offsets_back = list(range(1, REACH + 1)) + [-offset for offset in range(1, REACH + 1)]
    for offset in offsets_back:
        combined = combined + passed_along(
            grads_window[REACH - offset].astype(jnp.bfloat16), "ctx", -offset
        ).astype(jnp.float32)
    combined = combined.astype(jnp.bfloat16)
    dkey_s = combined[:, :head_cols]
    dvalue_s = combined[:, head_cols:]
    out_s = results[0].reshape(shard_rows, head_cols)
    dquery_s = results[1].reshape(shard_rows, head_cols)
    back = (
        lax.all_to_all(
            out_s.reshape(shard_rows, 1, head_cols), "head", split_axis=0, concat_axis=1, tiled=True
        ),
        lax.all_to_all(
            dquery_s.reshape(shard_rows, 1, head_cols),
            "head",
            split_axis=0,
            concat_axis=1,
            tiled=True,
        ),
        lax.all_to_all(
            dkey_s.reshape(shard_rows, 1, head_cols),
            "head",
            split_axis=0,
            concat_axis=1,
            tiled=True,
        ),
        lax.all_to_all(
            dvalue_s.reshape(shard_rows, 1, head_cols),
            "head",
            split_axis=0,
            concat_axis=1,
            tiled=True,
        ),
    )
    width = groups * head_cols
    return (
        back[0].reshape(tok_rows, width),
        back[1].reshape(tok_rows, width),
        back[2].reshape(tok_rows, width),
        back[3].reshape(tok_rows, width),
    )


def solution(mesh):
    return jax.shard_map(
        on_device,
        mesh=mesh,
        in_specs=(
            P(("ctx", "head"), None),
            P(("ctx", "head"), None),
            P(("ctx", "head"), None),
            P(("ctx", "head"), None),
            P(),
            P(),
        ),
        out_specs=(
            P(("ctx", "head"), None),
            P(("ctx", "head"), None),
            P(("ctx", "head"), None),
            P(("ctx", "head"), None),
        ),
        check_vma=False,
    )
```

profile of v0, /device:TPU:1, one launch (start us, length us, event | category | flops | bytes accessed | tf_op | source)
XLA Modules:
  0.0 304.3 jit_solution(11663556964533045326)
XLA Ops:
  2.5 10.2 %all-to-all-start.1 = ((bf16[128,16,64]{0,2,1:T(8,128)(2,1)}), bf16[128,16,64]{0,2,1:T(8,128)(2,1)S(1)}, u32[]{:S(2)}, u32[]{:S(2)}) async-start(bf16[128,16,64]{0,2,1:T(8,128)(2,1)} %bitcast.36), calls=%async_computation.1 | async-start | bytes 524288 | tf_op jit(solution)/shard_map/all_to_all | solution.py:43
  14.5 6.9 %all-to-all-done.1 = bf16[128,16,64]{0,2,1:T(8,128)(2,1)S(1)} async-done(((bf16[128,16,64]{0,2,1:T(8,128)(2,1)}), bf16[128,16,64]{0,2,1:T(8,128)(2,1)S(1)}, u32[]{:S(2)}, u32[]{:S(2)}) %all-to-all-start.1) | async-done | bytes 262176 | tf_op jit(solution)/shard_map/all_to_all | solution.py:43
  21.4 4.1 %all-to-all-start.2 = ((bf16[128,16,64]{0,2,1:T(8,128)(2,1)}), bf16[128,16,64]{0,2,1:T(8,128)(2,1)S(1)}, u32[]{:S(2)}, u32[]{:S(2)}) async-start(bf16[128,16,64]{0,2,1:T(8,128)(2,1)} %bitcast.39), calls=%async_computation.2 | async-start | bytes 524288 | tf_op jit(solution)/shard_map/all_to_all | solution.py:50
  25.7 8.6 %all-to-all-done.2 = bf16[128,16,64]{0,2,1:T(8,128)(2,1)S(1)} async-done(((bf16[128,16,64]{0,2,1:T(8,128)(2,1)}), bf16[128,16,64]{0,2,1:T(8,128)(2,1)S(1)}, u32[]{:S(2)}, u32[]{:S(2)}) %all-to-all-start.2) | async-done | bytes 262176 | tf_op jit(solution)/shard_map/all_to_all | solution.py:50
  38.7 4.2 %all-to-all-start = ((bf16[128,16,64]{0,2,1:T(8,128)(2,1)}), bf16[128,16,64]{0,2,1:T(8,128)(2,1)S(1)}, u32[]{:S(2)}, u32[]{:S(2)}) async-start(bf16[128,16,64]{0,2,1:T(8,128)(2,1)} %bitcast.31), calls=%async_computation | async-start | bytes 524288 | tf_op jit(solution)/shard_map/all_to_all | solution.py:36
  47.1 9.2 %collective-permute-start.3 = (bf16[2048,128]{0,1:T(8,128)(2,1)}, bf16[2048,128]{0,1:T(8,128)(2,1)}, u32[]{:S(2)}, u32[]{:S(2)}) collective-permute-start(bf16[2048,128]{0,1:T(8,128)(2,1)} %bitcast_dynamic-update-slice_fusion.1), channel_id=1, source_target_pairs={{0,480},{16,496},{32,0},{48,16},{64,32},{80,48},{96,64},{112,80},{... | collective-permute-start | bytes 1572872 | tf_op jit(solution)/shard_map/ppermute | solution.py:18
  56.3 3.9 %collective-permute-start.2 = (bf16[2048,128]{0,1:T(8,128)(2,1)}, bf16[2048,128]{0,1:T(8,128)(2,1)}, u32[]{:S(2)}, u32[]{:S(2)}) collective-permute-start(bf16[2048,128]{0,1:T(8,128)(2,1)} %bitcast_dynamic-update-slice_fusion.1), channel_id=1, source_target_pairs={{0,496},{16,0},{32,16},{48,32},{64,48},{80,64},{96,80},{112,96},{1... | collective-permute-start | bytes 1572872 | tf_op jit(solution)/shard_map/ppermute | solution.py:18
  61.3 7.2 %collective-permute-done.1 = bf16[2048,128]{0,1:T(8,128)(2,1)} collective-permute-done((bf16[2048,128]{0,1:T(8,128)(2,1)}, bf16[2048,128]{0,1:T(8,128)(2,1)}, u32[]{:S(2)}, u32[]{:S(2)}) %collective-permute-start.1) | collective-permute-done | bytes 524320 | tf_op jit(solution)/shard_map/ppermute | solution.py:18
  69.7 5.4 %all-to-all-start.3 = ((bf16[128,16,64]{0,2,1:T(8,128)(2,1)}), bf16[128,16,64]{0,2,1:T(8,128)(2,1)S(1)}, u32[]{:S(2)}, u32[]{:S(2)}) async-start(bf16[128,16,64]{0,2,1:T(8,128)(2,1)} %bitcast.223), calls=%async_computation.3 | async-start | bytes 524288 | tf_op jit(solution)/shard_map/all_to_all | solution.py:57
  75.1 7.5 %collective-permute-done.2 = bf16[2048,128]{0,1:T(8,128)(2,1)} collective-permute-done((bf16[2048,128]{0,1:T(8,128)(2,1)}, bf16[2048,128]{0,1:T(8,128)(2,1)}, u32[]{:S(2)}, u32[]{:S(2)}) %collective-permute-start.2) | collective-permute-done | bytes 524320 | tf_op jit(solution)/shard_map/ppermute | solution.py:18
  87.4 3.0 broadcast_in_dim.36
  90.4 108.7 %while.14 = (s32[]{:T(128)}, f32[80,128,128]{2,1,0:T(8,128)}, bf16[4,4,128,1,64]{2,4,1,3,0:T(8,128)(2,1)}, bf16[4,4,128,1,64]{2,4,1,3,0:T(8,128)(2,1)}, s32[4,4,...) while((s32[]{:T(128)}, f32[80,128,128]{2,1,0:T(8,128)}, ...), condition=%wide.region_5.6_spmd, body=%wide.region_0.5_spmd.sunk | while | flops 422641376 | bytes 45516148 | solution.py:144
  99.1 3.2 %copy.192 = f32[32,128,64]{2,1,0:T(8,128)} copy(f32[32,128,64]{1,2,0:T(8,128)} %bitcast.207) | data formatting | bytes 2097152 | tf_op jit(solution)/shard_map/while/body/eval_jaxpr/reshape | solution.py:136
  111.3 6.3 %scatter_fusion = f32[80,128,128]{2,1,0:T(8,128)} fusion(f32[80,128,128]{2,1,0:T(8,128)} %get-tuple-element.216, s32[32]{0:T(128)S(1)} %fusion.63, f32[32,128,128]{2,1,0:T(8,128)S(1)} %pad_maximum_fusion.2), kind=kCustom, calls=%fused_computation.1.clone.1 | custom fusion | flops 524288 | bytes 6291584 | tf_op jit(solution)/shard_map/while/body/eval_jaxpr/scatter-add | solution.py:140
  126.4 3.2 %copy.192 = f32[32,128,64]{2,1,0:T(8,128)} copy(f32[32,128,64]{1,2,0:T(8,128)} %bitcast.207) | data formatting | bytes 2097152 | tf_op jit(solution)/shard_map/while/body/eval_jaxpr/reshape | solution.py:136
  138.5 6.2 %scatter_fusion = f32[80,128,128]{2,1,0:T(8,128)} fusion(f32[80,128,128]{2,1,0:T(8,128)} %get-tuple-element.216, s32[32]{0:T(128)S(1)} %fusion.63, f32[32,128,128]{2,1,0:T(8,128)S(1)} %pad_maximum_fusion.2), kind=kCustom, calls=%fused_computation.1.clone.1 | custom fusion | flops 524288 | bytes 6291584 | tf_op jit(solution)/shard_map/while/body/eval_jaxpr/scatter-add | solution.py:140
  153.5 3.2 %copy.192 = f32[32,128,64]{2,1,0:T(8,128)} copy(f32[32,128,64]{1,2,0:T(8,128)} %bitcast.207) | data formatting | bytes 2097152 | tf_op jit(solution)/shard_map/while/body/eval_jaxpr/reshape | solution.py:136
  162.8 2.8 pad_maximum_fusion.2
  165.7 6.2 %scatter_fusion = f32[80,128,128]{2,1,0:T(8,128)} fusion(f32[80,128,128]{2,1,0:T(8,128)} %get-tuple-element.216, s32[32]{0:T(128)S(1)} %fusion.63, f32[32,128,128]{2,1,0:T(8,128)S(1)} %pad_maximum_fusion.2), kind=kCustom, calls=%fused_computation.1.clone.1 | custom fusion | flops 524288 | bytes 6291584 | tf_op jit(solution)/shard_map/while/body/eval_jaxpr/scatter-add | solution.py:140
  180.6 3.2 %copy.192 = f32[32,128,64]{2,1,0:T(8,128)} copy(f32[32,128,64]{1,2,0:T(8,128)} %bitcast.207) | data formatting | bytes 2097152 | tf_op jit(solution)/shard_map/while/body/eval_jaxpr/reshape | solution.py:136
  192.8 6.2 %scatter_fusion = f32[80,128,128]{2,1,0:T(8,128)} fusion(f32[80,128,128]{2,1,0:T(8,128)} %get-tuple-element.216, s32[32]{0:T(128)S(1)} %fusion.63, f32[32,128,128]{2,1,0:T(8,128)S(1)} %pad_maximum_fusion.2), kind=kCustom, calls=%fused_computation.1.clone.1 | custom fusion | flops 524288 | bytes 6291584 | tf_op jit(solution)/shard_map/while/body/eval_jaxpr/scatter-add | solution.py:140
  199.0 3.0 convert.6
  206.4 3.3 %collective-permute-start.5 = (bf16[2048,128]{0,1:T(8,128)(2,1)}, bf16[2048,128]{0,1:T(8,128)(2,1)S(1)}, u32[]{:S(2)}, u32[]{:S(2)}) collective-permute-start(bf16[2048,128]{0,1:T(8,128)(2,1)} %copy.170), channel_id=1, source_target_pairs={{0,480},{16,496},{32,0},{48,16},{64,32},{80,48},{96,64},{112,80},{... | collective-permute-start | bytes 1572872 | tf_op jit(solution)/shard_map/ppermute | solution.py:18
  213.6 5.7 %collective-permute-start.4 = (bf16[2048,128]{0,1:T(8,128)(2,1)}, bf16[2048,128]{0,1:T(8,128)(2,1)}, u32[]{:S(2)}, u32[]{:S(2)}) collective-permute-start(bf16[2048,128]{0,1:T(8,128)(2,1)} %copy.169), channel_id=1, source_target_pairs={{0,496},{16,0},{32,16},{48,32},{64,48},{80,64},{96,80},{112,96},{1... | collective-permute-start | bytes 1572872 | tf_op jit(solution)/shard_map/ppermute | solution.py:18
  221.7 11.5 %reduce.7 = bf16[2048,64]{1,0:T(8,128)(2,1)S(1)} reduce(bf16[2048,1,64]{2,1,0:T(2,128)(2,1)S(1)} %reshape.270, bf16[]{:T(256)} %broadcast.105), dimensions={1}, to_apply=%reshape.270.reduce_sub_computation | reduce | bytes 524290 | tf_op jit(solution)/shard_map/reshape;reshape | solution.py:162
  234.3 9.8 %all-to-all-start.5 = ((bf16[16,2,4096]{2,1,0:T(2,128)(2,1)}), bf16[16,2,4096]{2,1,0:T(2,128)(2,1)S(1)}, u32[]{:S(2)}, u32[]{:S(2)}) async-start(bf16[16,2,4096]{2,1,0:T(2,128)(2,1)} %reshape.273), calls=%async_computation.5 | async-start | bytes 524288 | tf_op jit(solution)/shard_map/all_to_all | solution.py:161
  245.6 11.5 %reduce.6 = bf16[2048,64]{1,0:T(8,128)(2,1)S(1)} reduce(bf16[2048,1,64]{2,1,0:T(2,128)(2,1)S(1)} %reshape.269, bf16[]{:T(256)} %broadcast.105), dimensions={1}, to_apply=%reshape.269.reduce_sub_computation | reduce | bytes 524290 | tf_op jit(solution)/shard_map/reshape;reshape | solution.py:159
  260.4 7.2 %all-to-all-start.4 = ((bf16[16,2,4096]{2,1,0:T(2,128)(2,1)}), bf16[16,2,4096]{2,1,0:T(2,128)(2,1)S(1)}, u32[]{:S(2)}, u32[]{:S(2)}) async-start(bf16[16,2,4096]{2,1,0:T(2,128)(2,1)} %reshape.271), calls=%async_computation.4 | async-start | bytes 524288 | tf_op jit(solution)/shard_map/all_to_all | solution.py:158
  269.9 6.5 %all-to-all-done.4 = bf16[16,2,4096]{2,1,0:T(2,128)(2,1)S(1)} async-done(((bf16[16,2,4096]{2,1,0:T(2,128)(2,1)}), bf16[16,2,4096]{2,1,0:T(2,128)(2,1)S(1)}, u32[]{:S(2)}, u32[]{:S(2)}) %all-to-all-start.4) | async-done | bytes 262176 | tf_op jit(solution)/shard_map/all_to_all | solution.py:158
  276.4 4.1 %all-to-all-start.7 = ((bf16[16,2,4096]{2,1,0:T(2,128)(2,1)}), bf16[16,2,4096]{2,1,0:T(2,128)(2,1)S(1)}, u32[]{:S(2)}, u32[]{:S(2)}) async-start(bf16[16,2,4096]{2,1,0:T(2,128)(2,1)} %reshape.277), calls=%async_computation.7 | async-start | bytes 524288 | tf_op jit(solution)/shard_map/all_to_all | solution.py:175
  282.6 6.6 %all-to-all-done.7 = bf16[16,2,4096]{2,1,0:T(2,128)(2,1)S(1)} async-done(((bf16[16,2,4096]{2,1,0:T(2,128)(2,1)}), bf16[16,2,4096]{2,1,0:T(2,128)(2,1)S(1)}, u32[]{:S(2)}, u32[]{:S(2)}) %all-to-all-start.7) | async-done | bytes 262176 | tf_op jit(solution)/shard_map/all_to_all | solution.py:175
  289.2 4.1 %all-to-all-start.6 = ((bf16[16,2,4096]{2,1,0:T(2,128)(2,1)}), bf16[16,2,4096]{2,1,0:T(2,128)(2,1)S(1)}, u32[]{:S(2)}, u32[]{:S(2)}) async-start(bf16[16,2,4096]{2,1,0:T(2,128)(2,1)} %reshape.275), calls=%async_computation.6 | async-start | bytes 524288 | tf_op jit(solution)/shard_map/all_to_all | solution.py:168
  (177 shorter events, 118.9 us)
Async XLA Ops:
  0.6 45.4 %copy-start = (s32[512,8]{0,1:T(8,128)S(1)}, s32[512,8]{0,1:T(8,128)}, u32[]{:S(2)}) copy-start(s32[512,8]{0,1:T(8,128)} %param.12) | copy-start | bytes 49156
  0.6 37.2 %copy-start.2 = (bf16[128,1024]{1,0:T(8,128)(2,1)S(1)}, bf16[128,1024]{1,0:T(8,128)(2,1)}, u32[]{:S(2)}) copy-start(bf16[128,1024]{1,0:T(8,128)(2,1)} %param.8) | copy-start | bytes 786436
  2.5 18.9 %all-to-all-start.1 = ((bf16[128,16,64]{0,2,1:T(8,128)(2,1)}), bf16[128,16,64]{0,2,1:T(8,128)(2,1)S(1)}, u32[]{:S(2)}, u32[]{:S(2)}) async-start(bf16[128,16,64]{0,2,1:T(8,128)(2,1)} %bitcast.36), calls=%async_computation.1 | async-start | bytes 524288 | tf_op jit(solution)/shard_map/all_to_all | solution.py:43
  12.7 33.6 %copy-start.3 = (bf16[128,1024]{1,0:T(8,128)(2,1)S(1)}, bf16[128,1024]{1,0:T(8,128)(2,1)}, u32[]{:S(2)}) copy-start(bf16[128,1024]{1,0:T(8,128)(2,1)} %param.11) | copy-start | bytes 786436
  21.4 12.9 %all-to-all-start.2 = ((bf16[128,16,64]{0,2,1:T(8,128)(2,1)}), bf16[128,16,64]{0,2,1:T(8,128)(2,1)S(1)}, u32[]{:S(2)}, u32[]{:S(2)}) async-start(bf16[128,16,64]{0,2,1:T(8,128)(2,1)} %bitcast.39), calls=%async_computation.2 | async-start | bytes 524288 | tf_op jit(solution)/shard_map/all_to_all | solution.py:50
  36.0 24.2 %collective-permute-start = (bf16[2048,128]{0,1:T(8,128)(2,1)}, bf16[2048,128]{0,1:T(8,128)(2,1)}, u32[]{:S(2)}, u32[]{:S(2)}) collective-permute-start(bf16[2048,128]{0,1:T(8,128)(2,1)} %bitcast_dynamic-update-slice_fusion.1), channel_id=1, source_target_pairs={{0,32},{16,48},{32,64},{48,80},{64,96},{80,112},{96,128},{112,144}... | collective-permute-start | bytes 1572872 | tf_op jit(solution)/shard_map/ppermute | solution.py:18
  38.7 31.0 %all-to-all-start = ((bf16[128,16,64]{0,2,1:T(8,128)(2,1)}), bf16[128,16,64]{0,2,1:T(8,128)(2,1)S(1)}, u32[]{:S(2)}, u32[]{:S(2)}) async-start(bf16[128,16,64]{0,2,1:T(8,128)(2,1)} %bitcast.31), calls=%async_computation | async-start | bytes 524288 | tf_op jit(solution)/shard_map/all_to_all | solution.py:36
  43.8 24.7 %collective-permute-start.1 = (bf16[2048,128]{0,1:T(8,128)(2,1)}, bf16[2048,128]{0,1:T(8,128)(2,1)}, u32[]{:S(2)}, u32[]{:S(2)}) collective-permute-start(bf16[2048,128]{0,1:T(8,128)(2,1)} %bitcast_dynamic-update-slice_fusion.1), channel_id=1, source_target_pairs={{0,16},{16,32},{32,48},{48,64},{64,80},{80,96},{96,112},{112,128},... | collective-permute-start | bytes 1572872 | tf_op jit(solution)/shard_map/ppermute | solution.py:18
  47.1 36.6 %collective-permute-start.3 = (bf16[2048,128]{0,1:T(8,128)(2,1)}, bf16[2048,128]{0,1:T(8,128)(2,1)}, u32[]{:S(2)}, u32[]{:S(2)}) collective-permute-start(bf16[2048,128]{0,1:T(8,128)(2,1)} %bitcast_dynamic-update-slice_fusion.1), channel_id=1, source_target_pairs={{0,480},{16,496},{32,0},{48,16},{64,32},{80,48},{96,64},{112,80},{... | collective-permute-start | bytes 1572872 | tf_op jit(solution)/shard_map/ppermute | solution.py:18
  56.3 26.3 %collective-permute-start.2 = (bf16[2048,128]{0,1:T(8,128)(2,1)}, bf16[2048,128]{0,1:T(8,128)(2,1)}, u32[]{:S(2)}, u32[]{:S(2)}) collective-permute-start(bf16[2048,128]{0,1:T(8,128)(2,1)} %bitcast_dynamic-update-slice_fusion.1), channel_id=1, source_target_pairs={{0,496},{16,0},{32,16},{48,32},{64,48},{80,64},{96,80},{112,96},{1... | collective-permute-start | bytes 1572872 | tf_op jit(solution)/shard_map/ppermute | solution.py:18
  69.7 17.7 %all-to-all-start.3 = ((bf16[128,16,64]{0,2,1:T(8,128)(2,1)}), bf16[128,16,64]{0,2,1:T(8,128)(2,1)S(1)}, u32[]{:S(2)}, u32[]{:S(2)}) async-start(bf16[128,16,64]{0,2,1:T(8,128)(2,1)} %bitcast.223), calls=%async_computation.3 | async-start | bytes 524288 | tf_op jit(solution)/shard_map/all_to_all | solution.py:57
  90.4 3.4 %copy-start.4 = (bf16[4,4,128,1,64]{2,4,1,3,0:T(8,128)(2,1)}, bf16[4,4,128,1,64]{2,4,1,3,0:T(8,128)(2,1)S(1)}, u32[]{:S(2)}) copy-start(bf16[4,4,128,1,64]{2,4,1,3,0:T(8,128)(2,1)S(1)} %get-tuple-element.233) | copy-start | bytes 786436 | tf_op jit(solution)/shard_map/while
  111.3 6.3 %copy-start.5 = (bf16[4,4,128,1,64]{2,4,1,3,0:T(8,128)(2,1)S(1)}, bf16[4,4,128,1,64]{2,4,1,3,0:T(8,128)(2,1)}, u32[]{:S(2)}) copy-start(bf16[4,4,128,1,64]{2,4,1,3,0:T(8,128)(2,1)} %copy-done.4) | copy-start | bytes 786436 | tf_op jit(solution)/shard_map/while
  117.6 3.4 %copy-start.4 = (bf16[4,4,128,1,64]{2,4,1,3,0:T(8,128)(2,1)}, bf16[4,4,128,1,64]{2,4,1,3,0:T(8,128)(2,1)S(1)}, u32[]{:S(2)}) copy-start(bf16[4,4,128,1,64]{2,4,1,3,0:T(8,128)(2,1)S(1)} %get-tuple-element.233) | copy-start | bytes 786436 | tf_op jit(solution)/shard_map/while
  138.5 6.2 %copy-start.5 = (bf16[4,4,128,1,64]{2,4,1,3,0:T(8,128)(2,1)S(1)}, bf16[4,4,128,1,64]{2,4,1,3,0:T(8,128)(2,1)}, u32[]{:S(2)}) copy-start(bf16[4,4,128,1,64]{2,4,1,3,0:T(8,128)(2,1)} %copy-done.4) | copy-start | bytes 786436 | tf_op jit(solution)/shard_map/while
  144.7 3.4 %copy-start.4 = (bf16[4,4,128,1,64]{2,4,1,3,0:T(8,128)(2,1)}, bf16[4,4,128,1,64]{2,4,1,3,0:T(8,128)(2,1)S(1)}, u32[]{:S(2)}) copy-start(bf16[4,4,128,1,64]{2,4,1,3,0:T(8,128)(2,1)S(1)} %get-tuple-element.233) | copy-start | bytes 786436 | tf_op jit(solution)/shard_map/while
  165.7 6.2 %copy-start.5 = (bf16[4,4,128,1,64]{2,4,1,3,0:T(8,128)(2,1)S(1)}, bf16[4,4,128,1,64]{2,4,1,3,0:T(8,128)(2,1)}, u32[]{:S(2)}) copy-start(bf16[4,4,128,1,64]{2,4,1,3,0:T(8,128)(2,1)} %copy-done.4) | copy-start | bytes 786436 | tf_op jit(solution)/shard_map/while
  171.9 3.4 %copy-start.4 = (bf16[4,4,128,1,64]{2,4,1,3,0:T(8,128)(2,1)}, bf16[4,4,128,1,64]{2,4,1,3,0:T(8,128)(2,1)S(1)}, u32[]{:S(2)}) copy-start(bf16[4,4,128,1,64]{2,4,1,3,0:T(8,128)(2,1)S(1)} %get-tuple-element.233) | copy-start | bytes 786436 | tf_op jit(solution)/shard_map/while
  192.8 6.2 %copy-start.5 = (bf16[4,4,128,1,64]{2,4,1,3,0:T(8,128)(2,1)S(1)}, bf16[4,4,128,1,64]{2,4,1,3,0:T(8,128)(2,1)}, u32[]{:S(2)}) copy-start(bf16[4,4,128,1,64]{2,4,1,3,0:T(8,128)(2,1)} %copy-done.4) | copy-start | bytes 786436 | tf_op jit(solution)/shard_map/while
  204.3 16.3 %copy-start.1 = (bf16[4,4,128,1,64]{2,4,1,3,0:T(8,128)(2,1)S(1)}, bf16[4,4,128,1,64]{2,4,1,3,0:T(8,128)(2,1)}, u32[]{:S(2)}) copy-start(bf16[4,4,128,1,64]{2,4,1,3,0:T(8,128)(2,1)} %get-tuple-element.54) | copy-start | bytes 786436
  206.4 52.3 %collective-permute-start.5 = (bf16[2048,128]{0,1:T(8,128)(2,1)}, bf16[2048,128]{0,1:T(8,128)(2,1)S(1)}, u32[]{:S(2)}, u32[]{:S(2)}) collective-permute-start(bf16[2048,128]{0,1:T(8,128)(2,1)} %copy.170), channel_id=1, source_target_pairs={{0,480},{16,496},{32,0},{48,16},{64,32},{80,48},{96,64},{112,80},{... | collective-permute-start | bytes 1572872 | tf_op jit(solution)/shard_map/ppermute | solution.py:18
  209.7 49.0 %collective-permute-start.6 = (bf16[2048,128]{0,1:T(8,128)(2,1)}, bf16[2048,128]{0,1:T(8,128)(2,1)}, u32[]{:S(2)}, u32[]{:S(2)}) collective-permute-start(bf16[2048,128]{0,1:T(8,128)(2,1)} %copy.171), channel_id=1, source_target_pairs={{0,16},{16,32},{32,48},{48,64},{64,80},{80,96},{96,112},{112,128},... | collective-permute-start | bytes 1572872 | tf_op jit(solution)/shard_map/ppermute | solution.py:18
  211.6 47.1 %collective-permute-start.7 = (bf16[2048,128]{0,1:T(8,128)(2,1)}, bf16[2048,128]{0,1:T(8,128)(2,1)}, u32[]{:S(2)}, u32[]{:S(2)}) collective-permute-start(bf16[2048,128]{0,1:T(8,128)(2,1)} %copy.172), channel_id=1, source_target_pairs={{0,32},{16,48},{32,64},{48,80},{64,96},{80,112},{96,128},{112,144}... | collective-permute-start | bytes 1572872 | tf_op jit(solution)/shard_map/ppermute | solution.py:18
  213.6 45.1 %collective-permute-start.4 = (bf16[2048,128]{0,1:T(8,128)(2,1)}, bf16[2048,128]{0,1:T(8,128)(2,1)}, u32[]{:S(2)}, u32[]{:S(2)}) collective-permute-start(bf16[2048,128]{0,1:T(8,128)(2,1)} %copy.169), channel_id=1, source_target_pairs={{0,496},{16,0},{32,16},{48,32},{64,48},{80,64},{96,80},{112,96},{1... | collective-permute-start | bytes 1572872 | tf_op jit(solution)/shard_map/ppermute | solution.py:18
  234.3 26.1 %all-to-all-start.5 = ((bf16[16,2,4096]{2,1,0:T(2,128)(2,1)}), bf16[16,2,4096]{2,1,0:T(2,128)(2,1)S(1)}, u32[]{:S(2)}, u32[]{:S(2)}) async-start(bf16[16,2,4096]{2,1,0:T(2,128)(2,1)} %reshape.273), calls=%async_computation.5 | async-start | bytes 524288 | tf_op jit(solution)/shard_map/all_to_all | solution.py:161
  260.4 15.9 %all-to-all-start.4 = ((bf16[16,2,4096]{2,1,0:T(2,128)(2,1)}), bf16[16,2,4096]{2,1,0:T(2,128)(2,1)S(1)}, u32[]{:S(2)}, u32[]{:S(2)}) async-start(bf16[16,2,4096]{2,1,0:T(2,128)(2,1)} %reshape.271), calls=%async_computation.4 | async-start | bytes 524288 | tf_op jit(solution)/shard_map/all_to_all | solution.py:158
  276.4 12.8 %all-to-all-start.7 = ((bf16[16,2,4096]{2,1,0:T(2,128)(2,1)}), bf16[16,2,4096]{2,1,0:T(2,128)(2,1)S(1)}, u32[]{:S(2)}, u32[]{:S(2)}) async-start(bf16[16,2,4096]{2,1,0:T(2,128)(2,1)} %reshape.277), calls=%async_computation.7 | async-start | bytes 524288 | tf_op jit(solution)/shard_map/all_to_all | solution.py:175
  289.2 12.9 %all-to-all-start.6 = ((bf16[16,2,4096]{2,1,0:T(2,128)(2,1)}), bf16[16,2,4096]{2,1,0:T(2,128)(2,1)S(1)}, u32[]{:S(2)}, u32[]{:S(2)}) async-start(bf16[16,2,4096]{2,1,0:T(2,128)(2,1)} %reshape.275), calls=%async_computation.6 | async-start | bytes 524288 | tf_op jit(solution)/shard_map/all_to_all | solution.py:168
where the time goes:
time: 307 us; the launch traced here: 304 us
  starting transfers between devices  79.2 us (26%)
  local copies, waits for them, and re-layouts  74.2 us (24%)
  other arithmetic  72.2 us (24%)
  waiting for transfers between devices  45.5 us (15%)
  matrix products  31.8 us (10%)
    ppermute x8, starting transfers between devices, passed_along(): return lax.ppermute(value, axis, pairs)  30.2 us
    scatter-add x4, other arithmetic, one_group(): totals = totals.at[chosen.reshape(-1)].add(joined)  24.9 us
    unnamed x37, local copies, waits for them, and re-layouts  20.5 us
    ppermute x8, waiting for transfers between devices, passed_along(): return lax.ppermute(value, axis, pairs)  14.8 us
    reshape x4, local copies, waits for them, and re-layouts, one_group(): dvalue_part.reshape(per_group * NNB, BLK, head_cols)  12.8 us
    gather x8, local copies, waits for them, and re-layouts, one_group(): selected = window[chosen]  12.6 us
    another operation x1, other arithmetic, on_device(): out_s.reshape(shard_rows, 1, head_cols)  11.5 us
    another operation x1, other arithmetic, on_device(): dquery_s.reshape(shard_rows, 1, head_cols)  11.5 us
  transfers between devices with their start and end apart: 16, of which 7 were waited for; matrix products, arithmetic and copies ran while one was open for 18% of the time, Pallas kernels for 0%

commit v1 on v0

v1 whole, which is shorter than its diff:
```python
import math

import jax
import jax.numpy as jnp
from jax import lax
from jax.experimental import pallas as pl
from jax.experimental.pallas import tpu as pltpu
from jax.sharding import Mesh, PartitionSpec as P

H = 16
E = 64
BLK = 128
NNB = 8
PLANES = 3
LOG2E = 1.4426950408889634

AXES = ("z", "yl", "yh", "x", "core")
HEADS = ("yl", "yh", "x")
VMEM = pltpu.VMEM


def pack_kernel(a_ref, b_ref, o_ref):
    for pair in range(H // 2):
        cols = slice(pair * 2 * E, (pair + 1) * 2 * E)
        a = a_ref[:, cols]
        b = b_ref[:, cols]
        o_ref[2 * pair] = jnp.concatenate([a[:, :E], b[:, :E]], axis=1)
        o_ref[2 * pair + 1] = jnp.concatenate([a[:, E:], b[:, E:]], axis=1)


def pack(a, b):
    rows = a.shape[0]
    return pl.pallas_call(
        pack_kernel,
        out_shape=jax.ShapeDtypeStruct((H, rows, 2 * E), a.dtype),
        in_specs=[pl.BlockSpec(memory_space=VMEM)] * 2,
        out_specs=pl.BlockSpec(memory_space=VMEM),
        name="pack",
    )(a, b)


def unpack_kernel(i_ref, a_ref, b_ref):
    for pair in range(H // 2):
        cols = slice(pair * 2 * E, (pair + 1) * 2 * E)
        even = i_ref[2 * pair]
        odd = i_ref[2 * pair + 1]
        a_ref[:, cols] = jnp.concatenate([even[:, :E], odd[:, :E]], axis=1)
        b_ref[:, cols] = jnp.concatenate([even[:, E:], odd[:, E:]], axis=1)


def unpack(joined):
    rows = joined.shape[1]
    shape = jax.ShapeDtypeStruct((rows, H * E), joined.dtype)
    return pl.pallas_call(
        unpack_kernel,
        out_shape=(shape, shape),
        in_specs=[pl.BlockSpec(memory_space=VMEM)],
        out_specs=[pl.BlockSpec(memory_space=VMEM)] * 2,
        name="unpack",
    )(joined)


def attend_block(s, slots, used, index_of, qg_ref, win, acc, st, oq_ref):
    qg = qg_ref[s]
    low = lax.broadcasted_iota(jnp.int32, (BLK, 2 * E), 1) < E
    zero = jnp.zeros_like(qg)
    both = jnp.concatenate(
        [jnp.where(low, qg * jnp.bfloat16(0.125), zero), jnp.where(low, zero, qg)], axis=0
    )
    where = [index_of(j) for j in range(slots)]
    highest = None
    for j in range(slots):
        pair = lax.dot_general(
            win[where[j]], both, (((1,), (1,)), ((), ())), preferred_element_type=jnp.float32
        )
        scores = pair[:, :BLK]
        if j == slots - 1:
            scores = jnp.where(j < used, scores, -1e30)
        st[j, :, :BLK] = scores
        st[j, :, BLK:] = pair[:, BLK:]
        top = jnp.max(scores, axis=0, keepdims=True)
        highest = top if highest is None else jnp.maximum(highest, top)
    total = jnp.zeros((1, BLK), jnp.float32)
    mixed = jnp.zeros((1, BLK), jnp.float32)
    for j in range(slots):
        raised = jnp.exp2((st[j, :, :BLK] - highest) * LOG2E)
        st[j, :, :BLK] = raised
        total = total + jnp.sum(raised, axis=0, keepdims=True)
        mixed = mixed + jnp.sum(raised * st[j, :, BLK:], axis=0, keepdims=True)
    inverse = 1.0 / total
    delta = mixed * inverse
    sums = None
    for j in range(slots):
        probability = st[j, :, :BLK] * inverse
        dscore = probability * (st[j, :, BLK:] - delta)
        joined = jnp.concatenate(
            [dscore.astype(jnp.bfloat16), probability.astype(jnp.bfloat16)], axis=1
        )
        acc[where[j]] += jnp.dot(joined, both, preferred_element_type=jnp.float32)
        part = jnp.dot(win[where[j]].T, joined, preferred_element_type=jnp.float32)
        sums = part if sums is None else sums + part
    result = jnp.concatenate([sums[:E, :BLK] * 0.125, sums[E:, BLK:]], axis=0)
    oq_ref[s] = result.T.astype(oq_ref.dtype)


def attend_kernel(
    place, variants, nbr, cnt, qg_ref, *rest
):
    kv_refs = rest[:6]
    oq_ref, own_ref, other_ref = rest[6:9]
    win, acc, st, sems = rest[9:]
    z, core = place()
    blocks = qg_ref.shape[0]
    plane_blocks = 2 * blocks
    all_blocks = cnt.shape[0]
    copies = [
        pltpu.make_async_copy(kv_refs[i], win.at[pl.ds(i * blocks, blocks)], sems.at[i])
        for i in range(6)
    ]
    for copy in copies:
        copy.start()
    first = (z - 1) * plane_blocks

    @pl.loop(0, 6 * blocks)
    def _(i):
        acc[i] = jnp.zeros_like(acc[i])

    for copy in copies:
        copy.wait()

    @pl.loop(0, blocks)
    def _(s):
        b = z * plane_blocks + 2 * s + core
        used = cnt[b]

        def index_of(j):
            rel = lax.rem(nbr[j, b] - first + all_blocks, all_blocks)
            side = lax.rem(rel + core, 2)
            return side * (PLANES * blocks) + lax.div(rel, 2)

        before = 0
        for slots in variants:

            @pl.when((used > before) & (used <= slots))
            def _(slots=slots):
                attend_block(s, slots, used, index_of, qg_ref, win, acc, st, oq_ref)

            before = slots

    own_ref[...] = acc[pl.ds(0, PLANES * blocks)]

    @pl.loop(0, PLANES * blocks)
    def _(i):
        other_ref[i] = acc[PLANES * blocks + i].astype(other_ref.dtype)


def attend(place, nbr_t, counts, qg, kvs, variants=(2, 4, 6, 8)):
    import functools

    blocks = qg.shape[0]
    tile = (BLK, 2 * E)
    return pl.pallas_call(
        functools.partial(attend_kernel, place, variants),
        out_shape=(
            jax.ShapeDtypeStruct((blocks,) + tile, jnp.bfloat16),
            jax.ShapeDtypeStruct((PLANES * blocks,) + tile, jnp.float32),
            jax.ShapeDtypeStruct((PLANES * blocks,) + tile, jnp.bfloat16),
        ),
        in_specs=[pl.BlockSpec(memory_space=pltpu.SMEM)] * 2
        + [pl.BlockSpec(memory_space=VMEM)]
        + [pl.BlockSpec(memory_space=pl.ANY)] * 6,
        out_specs=[pl.BlockSpec(memory_space=VMEM)] * 3,
        scratch_shapes=[
            pltpu.VMEM((6 * blocks,) + tile, jnp.bfloat16),
            pltpu.VMEM((6 * blocks,) + tile, jnp.float32),
            pltpu.VMEM((NNB, BLK, 2 * BLK), jnp.float32),
            pltpu.SemaphoreType.DMA((6,)),
        ],
        compiler_params=pltpu.CompilerParams(vmem_limit_bytes=40 << 20),
        cost_estimate=pl.CostEstimate(
            flops=2 * 5 * blocks * 5 * BLK * BLK * E,
            bytes_accessed=8 << 20,
            transcendentals=blocks * 5 * BLK * BLK,
        ),
        name="attend",
    )(nbr_t, counts, qg, *kvs)


def on_device(query, key, value, grad_out, neighbour, counts):
    planes = lax.axis_size("z")
    up = [(i, (i + 1) % planes) for i in range(planes)]
    down = [(i, (i - 1) % planes) for i in range(planes)]
    swap = [(0, 1), (1, 0)]

    def exchange(packed):
        return lax.all_to_all(packed, HEADS, split_axis=0, concat_axis=0, tiled=True)

    kv = exchange(pack(key, value))
    kv_before = lax.ppermute(kv, "z", up)
    kv_after = lax.ppermute(kv, "z", down)
    qg = exchange(pack(query, grad_out))
    kv_other = lax.ppermute(kv, "core", swap)
    before_other = lax.ppermute(kv_before, "core", swap)
    after_other = lax.ppermute(kv_after, "core", swap)

    def place():
        return lax.axis_index("z"), lax.axis_index("core")

    oq, own, other = attend(
        place,
        neighbour.T,
        counts,
        qg,
        (kv_before, kv, kv_after, before_other, kv_other, after_other),
    )
    blocks = qg.shape[0]
    mine = lax.ppermute(other, "core", swap)
    sums = own + mine.astype(jnp.float32)
    to_before = sums[:blocks].astype(jnp.bfloat16)
    to_after = sums[2 * blocks :].astype(jnp.bfloat16)
    from_after = lax.ppermute(to_before, "z", down)
    from_before = lax.ppermute(to_after, "z", up)
    back_oq = exchange(oq)
    total = (
        sums[blocks : 2 * blocks]
        + from_after.astype(jnp.float32)
        + from_before.astype(jnp.float32)
    ).astype(jnp.bfloat16)
    dquery, out = unpack(back_oq)
    dkey, dvalue = unpack(exchange(total))
    return out, dquery, dkey, dvalue


def solution(mesh):
    inner = Mesh(mesh.devices.reshape(16, 2, 2, 4, 2), AXES)
    return jax.shard_map(
        on_device,
        mesh=inner,
        in_specs=(P(AXES, None),) * 4 + (P(), P()),
        out_specs=(P(AXES, None),) * 4,
        check_vma=False,
    )
```

time: 307 us -> 130 us (0.42)
  local copies, waits for them, and re-layouts: 74.2 us -> 1.9 us
  other arithmetic: 72.2 us -> 2.87 us
  starting transfers between devices: 79.2 us -> 42.9 us
  matrix products: 31.8 us -> 0 us
  blocking collectives: 0 us -> 31.6 us
  Pallas kernels: 0 us -> 24.5 us
  waiting for transfers between devices: 45.5 us -> 24.4 us
    all_to_all x8 -> x2, starting transfers between devices: 49.1 us -> 7.83 us  [exchange(): lax.all_to_all(packed, HEADS, split_axis=0, concat_axis=0, tiled=True)]
    dot_general x24 -> x0, matrix products: 31.8 us -> none  [the longest x4 10.5 us: one_group(): jnp.einsum('rhijt,rihe->rjthe', weights, cotangent, preferred_element_typ...]
    all_to_all x0 -> x2, blocking collectives: none -> 31.6 us  [exchange(): lax.all_to_all(packed, HEADS, split_axis=0, concat_axis=0, tiled=True)]
    another operation x5 -> x1, other arithmetic: 26.1 us -> 0.67 us  [the longest x1 11.5 us: on_device(): out_s.reshape(shard_rows, 1, head_cols)]
    scatter-add x4 -> x0, other arithmetic: 24.9 us -> none  [one_group(): totals = totals.at[chosen.reshape(-1)].add(joined)]
    pallas_call x0 -> x5, Pallas kernels: none -> 24.5 us  [the longest x1 16.4 us: attend(): pl.pallas_call(functools.partial(attend_kernel, place, variants), out_sha...]
    all_to_all x8 -> x2, waiting for transfers between devices: 30.8 us -> 8.18 us  [exchange(): lax.all_to_all(packed, HEADS, split_axis=0, concat_axis=0, tiled=True)]
    reshape x14 -> x0, local copies, waits for them, and re-layouts: 21 us -> none  [the longest x4 12.8 us: one_group(): dvalue_part.reshape(per_group * NNB, BLK, head_cols)]
  transfers between devices with their start and end apart: 16 -> 10, of which waited for: 7 -> 7; matrix products, arithmetic and copies ran while one was open for 18% -> 2% of each run, Pallas kernels for 0% -> 3%
where the time goes in v1:
time: 130 us; the launch traced here: 129 us
  starting transfers between devices  42.9 us (33%)
  blocking collectives  31.6 us (24%)
  Pallas kernels  24.5 us (19%)
  waiting for transfers between devices  24.4 us (19%)
  other arithmetic  2.87 us (2%)
  local copies, waits for them, and re-layouts  1.9 us (1%)
    all_to_all x2, blocking collectives, exchange(): lax.all_to_all(packed, HEADS, split_axis=0, concat_axis=0, tiled=True)  31.6 us
    pallas_call x1, Pallas kernels, attend(): pl.pallas_call(functools.partial(attend_kernel, place, variants), out_sha...  16.4 us
    ppermute x1, starting transfers between devices, on_device(): kv_after = lax.ppermute(kv, 'z', down)  12.6 us
    all_to_all x2, waiting for transfers between devices, exchange(): lax.all_to_all(packed, HEADS, split_axis=0, concat_axis=0, tiled=True)  8.18 us
    all_to_all x2, starting transfers between devices, exchange(): lax.all_to_all(packed, HEADS, split_axis=0, concat_axis=0, tiled=True)  7.83 us
    ppermute x1, waiting for transfers between devices, on_device(): from_after = lax.ppermute(to_before, 'z', down)  5.99 us
    ppermute x1, starting transfers between devices, on_device(): before_other = lax.ppermute(kv_before, 'core', swap)  4.8 us
    ppermute x1, starting transfers between devices, on_device(): after_other = lax.ppermute(kv_after, 'core', swap)  4.52 us
  transfers between devices with their start and end apart: 10, of which 7 were waited for; matrix products, arithmetic and copies ran while one was open for 2% of the time, Pallas kernels for 3%

profile of v1, /device:TPU:1, one launch (start us, length us, event | category | flops | bytes accessed | tf_op | source)
XLA Modules:
  0.0 129.0 jit_solution(4861523648533071784)
XLA Ops:
  0.7 2.0 %pack.3 = bf16[16,128,128]{2,1,0:T(8,128)(2,1)} custom-call(bf16[128,1024]{1,0:T(8,128)(2,1)} %a_ref.3, bf16[128,1024]{1,0:T(8,128)(2,1)} %b_ref.3), custom_call_target="tpu_custom_call" | custom-call | tf_op jit(solution)/shard_map/pack/pallas_call | solution.py:33
  2.7 16.8 %all_to_all.20.rest_1_ = bf16[16,128,128]{2,1,0:T(8,128)(2,1)S(1)} all-to-all(bf16[16,128,128]{2,1,0:T(8,128)(2,1)} %pack.3), channel_id=1, replica_groups=mesh['z'=16,'yl'=2,'yh'=2,'x'=4,'core'=2] {'yl','yh','x'}, dimensions={0} | all-to-all | bytes 1048576 | tf_op jit(solution)/shard_map/all_to_all | solution.py:196
  19.5 12.6 %collective-permute-start.1 = (bf16[16,128,128]{2,1,0:T(8,128)(2,1)S(1)}, bf16[16,128,128]{2,1,0:T(8,128)(2,1)S(1)}, u32[]{:S(2)}, u32[]{:S(2)}) collective-permute-start(bf16[16,128,128]{2,1,0:T(8,128)(2,1)S(1)} %all_to_all.20.rest_1_), channel_id=1, source_target_pairs={{0,480},{32,0},{64,32},{96,64},{128,96},{160,128},{192,160},{224,1... | collective-permute-start | bytes 1572872 | tf_op jit(solution)/shard_map/ppermute | solution.py:200
  32.1 1.9 %collective-permute-start = (bf16[16,128,128]{2,1,0:T(8,128)(2,1)S(1)}, bf16[16,128,128]{2,1,0:T(8,128)(2,1)S(1)}, u32[]{:S(2)}, u32[]{:S(2)}) collective-permute-start(bf16[16,128,128]{2,1,0:T(8,128)(2,1)S(1)} %all_to_all.20.rest_1_), channel_id=1, source_target_pairs={{0,32},{32,64},{64,96},{96,128},{128,160},{160,192},{192,224},{224... | collective-permute-start | bytes 1572872 | tf_op jit(solution)/shard_map/ppermute | solution.py:199
  34.0 4.0 %collective-permute-start.3 = (bf16[16,128,128]{2,1,0:T(8,128)(2,1)S(1)}, bf16[16,128,128]{2,1,0:T(8,128)(2,1)S(1)}, u32[]{:S(2)}, u32[]{:S(2)}) collective-permute-start(bf16[16,128,128]{2,1,0:T(8,128)(2,1)S(1)} %all_to_all.20.rest_1_), channel_id=1, source_target_pairs={{0,1},{1,0},{2,3},{3,2},{4,5},{5,4},{6,7},{7,6},{8,9},{9,8},{10,11... | collective-permute-start | bytes 1572872 | tf_op jit(solution)/shard_map/ppermute | solution.py:202
  38.0 3.6 %collective-permute-done.1.rest_2_ = bf16[16,128,128]{2,1,0:T(8,128)(2,1)S(1)} collective-permute-done((bf16[16,128,128]{2,1,0:T(8,128)(2,1)S(1)}, bf16[16,128,128]{2,1,0:T(8,128)(2,1)S(1)}, u32[]{:S(2)}, u32[]{:S(2)}) %collective-permute-start.1) | collective-permute-done | bytes 524320 | tf_op jit(solution)/shard_map/ppermute | solution.py:200
  41.6 4.5 %collective-permute-start.4 = (bf16[16,128,128]{2,1,0:T(8,128)(2,1)S(1)}, bf16[16,128,128]{2,1,0:T(8,128)(2,1)S(1)}, u32[]{:S(2)}, u32[]{:S(2)}) collective-permute-start(bf16[16,128,128]{2,1,0:T(8,128)(2,1)S(1)} %collective-permute-done.1.rest_2_), channel_id=1, source_target_pairs={{0,1},{1,0},{2,3},{3,2},{4,5},{5,4},{6,7},{7,6},{8,9},{9,8},{10,11... | collective-permute-start | bytes 1572872 | tf_op jit(solution)/shard_map/ppermute | solution.py:204
  46.1 0.5 collective-permute-done.rest_0_
  46.6 4.8 %collective-permute-start.2 = (bf16[16,128,128]{2,1,0:T(8,128)(2,1)S(1)}, bf16[16,128,128]{2,1,0:T(8,128)(2,1)S(1)}, u32[]{:S(2)}, u32[]{:S(2)}) collective-permute-start(bf16[16,128,128]{2,1,0:T(8,128)(2,1)S(1)} %collective-permute-done.rest_0_), channel_id=1, source_target_pairs={{0,1},{1,0},{2,3},{3,2},{4,5},{5,4},{6,7},{7,6},{8,9},{9,8},{10,11... | collective-permute-start | bytes 1572872 | tf_op jit(solution)/shard_map/ppermute | solution.py:203
  51.4 2.0 %pack.2 = bf16[16,128,128]{2,1,0:T(8,128)(2,1)} custom-call(bf16[128,1024]{1,0:T(8,128)(2,1)} %a_ref.2, bf16[128,1024]{1,0:T(8,128)(2,1)} %b_ref.2), custom_call_target="tpu_custom_call" | custom-call | tf_op jit(solution)/shard_map/pack/pallas_call | solution.py:33
  53.5 14.8 %all_to_all.21.qg_ref = bf16[16,128,128]{2,1,0:T(8,128)(2,1)S(1)} all-to-all(bf16[16,128,128]{2,1,0:T(8,128)(2,1)} %pack.2), channel_id=1, replica_groups=mesh['z'=16,'yl'=2,'yh'=2,'x'=4,'core'=2] {'yl','yh','x'}, dimensions={0} | all-to-all | bytes 1048576 | tf_op jit(solution)/shard_map/all_to_all | solution.py:196
  68.3 0.0 collective-permute-done.3.rest_4_
  68.3 0.0 collective-permute-done.4.rest_5_
  68.3 0.0 collective-permute-done.2.rest_3_
  68.4 16.4 %attend.1 = (bf16[16,128,128]{2,1,0:T(8,128)(2,1)S(1)}, f32[48,128,128]{2,1,0:T(8,128)S(1)}, bf16[48,128,128]{2,1,0:T(8,128)(2,1)S(1)}) custom-call(s32[8,512]{1,0:T(8,128)S(1)} %bitcast.1, s32[512]{0:T(512)S(1)} %copy-done.2, bf16[16,128,128]{2,1,0:T(8,128)(2,1)S(1)} %all_to_all.21.qg_ref, bf16[16,128,128]{2,1,0:T(8,128)(2,1)S(1)} %collective-permute-done.rest_0_, ...), custom_call_target="tpu_custom_call" | custom-call | flops 838860800 | bytes 8388608 | tf_op jit(solution)/shard_map/attend/pallas_call | solution.py:162
  84.8 1.9 %collective-permute-start.5 = (bf16[48,128,128]{2,1,0:T(8,128)(2,1)S(1)}, bf16[48,128,128]{2,1,0:T(8,128)(2,1)S(1)}, u32[]{:S(2)}, u32[]{:S(2)}) collective-permute-start(bf16[48,128,128]{2,1,0:T(8,128)(2,1)S(1)} %get-tuple-element.15), channel_id=1, source_target_pairs={{0,1},{1,0},{2,3},{3,2},{4,5},{5,4},{6,7},{7,6},{8,9},{9,8},{10,11... | collective-permute-start | bytes 4718600 | tf_op jit(solution)/shard_map/ppermute | solution.py:217
  86.7 3.4 %collective-permute-done.5 = bf16[48,128,128]{2,1,0:T(8,128)(2,1)S(1)} collective-permute-done((bf16[48,128,128]{2,1,0:T(8,128)(2,1)S(1)}, bf16[48,128,128]{2,1,0:T(8,128)(2,1)S(1)}, u32[]{:S(2)}, u32[]{:S(2)}) %collective-permute-start.5) | collective-permute-done | bytes 1572896 | tf_op jit(solution)/shard_map/ppermute | solution.py:217
  90.1 0.7 fusion.2
  90.8 0.0 copy-done
  90.8 1.1 fusion.3
  91.9 2.0 %collective-permute-start.6 = (bf16[16,128,128]{2,1,0:T(8,128)(2,1)}, bf16[16,128,128]{2,1,0:T(8,128)(2,1)}, u32[]{:S(2)}, u32[]{:S(2)}) collective-permute-start(bf16[16,128,128]{2,1,0:T(8,128)(2,1)} %get-tuple-element.20), channel_id=1, source_target_pairs={{0,480},{32,0},{64,32},{96,64},{128,96},{160,128},{192,160},{224,1... | collective-permute-start | bytes 1572872 | tf_op jit(solution)/shard_map/ppermute | solution.py:221
  93.9 3.3 %collective-permute-start.7 = (bf16[16,128,128]{2,1,0:T(8,128)(2,1)}, bf16[16,128,128]{2,1,0:T(8,128)(2,1)}, u32[]{:S(2)}, u32[]{:S(2)}) collective-permute-start(bf16[16,128,128]{2,1,0:T(8,128)(2,1)} %get-tuple-element.21), channel_id=1, source_target_pairs={{0,32},{32,64},{64,96},{96,128},{128,160},{160,192},{192,224},{224... | collective-permute-start | bytes 1572872 | tf_op jit(solution)/shard_map/ppermute | solution.py:222
  97.1 4.3 %all-to-all-start.2 = ((bf16[16,128,128]{2,1,0:T(8,128)(2,1)}), bf16[16,128,128]{2,1,0:T(8,128)(2,1)}, u32[]{:S(2)}, u32[]{:S(2)}) async-start(bf16[16,128,128]{2,1,0:T(8,128)(2,1)} %copy-done), calls=%async_computation.2 | async-start | bytes 1048576 | tf_op jit(solution)/shard_map/all_to_all | solution.py:196
  101.4 6.0 %collective-permute-done.6 = bf16[16,128,128]{2,1,0:T(8,128)(2,1)} collective-permute-done((bf16[16,128,128]{2,1,0:T(8,128)(2,1)}, bf16[16,128,128]{2,1,0:T(8,128)(2,1)}, u32[]{:S(2)}, u32[]{:S(2)}) %collective-permute-start.6) | collective-permute-done | bytes 524320 | tf_op jit(solution)/shard_map/ppermute | solution.py:221
  107.4 2.7 %collective-permute-done.7 = bf16[16,128,128]{2,1,0:T(8,128)(2,1)} collective-permute-done((bf16[16,128,128]{2,1,0:T(8,128)(2,1)}, bf16[16,128,128]{2,1,0:T(8,128)(2,1)}, u32[]{:S(2)}, u32[]{:S(2)}) %collective-permute-start.7) | collective-permute-done | bytes 524320 | tf_op jit(solution)/shard_map/ppermute | solution.py:222
  110.1 2.2 %fusion.1 = bf16[16,128,128]{2,1,0:T(8,128)(2,1)} fusion(f32[48,128,128]{2,1,0:T(8,128)S(1)} %get-tuple-element.19, bf16[16,128,128]{2,1,0:T(8,128)(2,1)} %collective-permute-done.7, bf16[16,128,128]{2,1,0:T(8,128)(2,1)} %collective-permute-done.6), kind=kLoop, calls=%fused_computation.3 | loop fusion | flops 1310720 | bytes 2621440 | tf_op jit(solution)/shard_map/convert_element_type | solution.py:228
  112.3 0.1 all-to-all-done.2.i_ref
  112.4 3.6 %all-to-all-start.3 = ((bf16[16,128,128]{2,1,0:T(8,128)(2,1)}), bf16[16,128,128]{2,1,0:T(8,128)(2,1)S(1)}, u32[]{:S(2)}, u32[]{:S(2)}) async-start(bf16[16,128,128]{2,1,0:T(8,128)(2,1)} %fusion.1), calls=%async_computation.3 | async-start | bytes 1048576 | tf_op jit(solution)/shard_map/all_to_all | solution.py:196
  116.0 2.0 %unpack.2 = (bf16[128,1024]{1,0:T(8,128)(2,1)}, bf16[128,1024]{1,0:T(8,128)(2,1)}) custom-call(bf16[16,128,128]{2,1,0:T(8,128)(2,1)} %all-to-all-done.2.i_ref), custom_call_target="tpu_custom_call" | custom-call | tf_op jit(solution)/shard_map/unpack/pallas_call | solution.py:54
  118.0 8.1 %all-to-all-done.3.i_ref = bf16[16,128,128]{2,1,0:T(8,128)(2,1)S(1)} async-done(((bf16[16,128,128]{2,1,0:T(8,128)(2,1)}), bf16[16,128,128]{2,1,0:T(8,128)(2,1)S(1)}, u32[]{:S(2)}, u32[]{:S(2)}) %all-to-all-start.3) | async-done | bytes 524320 | tf_op jit(solution)/shard_map/all_to_all | solution.py:196
  126.1 0.8 copy-done.3
  126.9 2.0 %unpack.3 = (bf16[128,1024]{1,0:T(8,128)(2,1)}, bf16[128,1024]{1,0:T(8,128)(2,1)}) custom-call(bf16[16,128,128]{2,1,0:T(8,128)(2,1)} %copy-done.3), custom_call_target="tpu_custom_call" | custom-call | tf_op jit(solution)/shard_map/unpack/pallas_call | solution.py:54
  (6 shorter events, 0.0 us)
Async XLA Ops:
  0.6 67.7 %copy-start.2 = (s32[512]{0:T(512)S(1)}, s32[512]{0:T(512)}, u32[]{:S(2)}) copy-start(s32[512]{0:T(512)} %cnt.1) | copy-start | bytes 6148
  0.6 67.7 %copy-start.1 = (s32[512,8]{0,1:T(8,128)S(1)}, s32[512,8]{0,1:T(8,128)}, u32[]{:S(2)}) copy-start(s32[512,8]{0,1:T(8,128)} %param.10) | copy-start | bytes 49156
  19.5 22.1 %collective-permute-start.1 = (bf16[16,128,128]{2,1,0:T(8,128)(2,1)S(1)}, bf16[16,128,128]{2,1,0:T(8,128)(2,1)S(1)}, u32[]{:S(2)}, u32[]{:S(2)}) collective-permute-start(bf16[16,128,128]{2,1,0:T(8,128)(2,1)S(1)} %all_to_all.20.rest_1_), channel_id=1, source_target_pairs={{0,480},{32,0},{64,32},{96,64},{128,96},{160,128},{192,160},{224,1... | collective-permute-start | bytes 1572872 | tf_op jit(solution)/shard_map/ppermute | solution.py:200
  32.1 14.5 %collective-permute-start = (bf16[16,128,128]{2,1,0:T(8,128)(2,1)S(1)}, bf16[16,128,128]{2,1,0:T(8,128)(2,1)S(1)}, u32[]{:S(2)}, u32[]{:S(2)}) collective-permute-start(bf16[16,128,128]{2,1,0:T(8,128)(2,1)S(1)} %all_to_all.20.rest_1_), channel_id=1, source_target_pairs={{0,32},{32,64},{64,96},{96,128},{128,160},{160,192},{192,224},{224... | collective-permute-start | bytes 1572872 | tf_op jit(solution)/shard_map/ppermute | solution.py:199
  34.0 34.3 %collective-permute-start.3 = (bf16[16,128,128]{2,1,0:T(8,128)(2,1)S(1)}, bf16[16,128,128]{2,1,0:T(8,128)(2,1)S(1)}, u32[]{:S(2)}, u32[]{:S(2)}) collective-permute-start(bf16[16,128,128]{2,1,0:T(8,128)(2,1)S(1)} %all_to_all.20.rest_1_), channel_id=1, source_target_pairs={{0,1},{1,0},{2,3},{3,2},{4,5},{5,4},{6,7},{7,6},{8,9},{9,8},{10,11... | collective-permute-start | bytes 1572872 | tf_op jit(solution)/shard_map/ppermute | solution.py:202
  41.6 26.7 %collective-permute-start.4 = (bf16[16,128,128]{2,1,0:T(8,128)(2,1)S(1)}, bf16[16,128,128]{2,1,0:T(8,128)(2,1)S(1)}, u32[]{:S(2)}, u32[]{:S(2)}) collective-permute-start(bf16[16,128,128]{2,1,0:T(8,128)(2,1)S(1)} %collective-permute-done.1.rest_2_), channel_id=1, source_target_pairs={{0,1},{1,0},{2,3},{3,2},{4,5},{5,4},{6,7},{7,6},{8,9},{9,8},{10,11... | collective-permute-start | bytes 1572872 | tf_op jit(solution)/shard_map/ppermute | solution.py:204
  46.6 21.7 %collective-permute-start.2 = (bf16[16,128,128]{2,1,0:T(8,128)(2,1)S(1)}, bf16[16,128,128]{2,1,0:T(8,128)(2,1)S(1)}, u32[]{:S(2)}, u32[]{:S(2)}) collective-permute-start(bf16[16,128,128]{2,1,0:T(8,128)(2,1)S(1)} %collective-permute-done.rest_0_), channel_id=1, source_target_pairs={{0,1},{1,0},{2,3},{3,2},{4,5},{5,4},{6,7},{7,6},{8,9},{9,8},{10,11... | collective-permute-start | bytes 1572872 | tf_op jit(solution)/shard_map/ppermute | solution.py:203
  84.8 6.0 %copy-start = (bf16[16,128,128]{2,1,0:T(8,128)(2,1)}, bf16[16,128,128]{2,1,0:T(8,128)(2,1)S(1)}, u32[]{:S(2)}) copy-start(bf16[16,128,128]{2,1,0:T(8,128)(2,1)S(1)} %get-tuple-element.11) | copy-start | bytes 1572868
  84.8 5.3 %collective-permute-start.5 = (bf16[48,128,128]{2,1,0:T(8,128)(2,1)S(1)}, bf16[48,128,128]{2,1,0:T(8,128)(2,1)S(1)}, u32[]{:S(2)}, u32[]{:S(2)}) collective-permute-start(bf16[48,128,128]{2,1,0:T(8,128)(2,1)S(1)} %get-tuple-element.15), channel_id=1, source_target_pairs={{0,1},{1,0},{2,3},{3,2},{4,5},{5,4},{6,7},{7,6},{8,9},{9,8},{10,11... | collective-permute-start | bytes 4718600 | tf_op jit(solution)/shard_map/ppermute | solution.py:217
  91.9 15.5 %collective-permute-start.6 = (bf16[16,128,128]{2,1,0:T(8,128)(2,1)}, bf16[16,128,128]{2,1,0:T(8,128)(2,1)}, u32[]{:S(2)}, u32[]{:S(2)}) collective-permute-start(bf16[16,128,128]{2,1,0:T(8,128)(2,1)} %get-tuple-element.20), channel_id=1, source_target_pairs={{0,480},{32,0},{64,32},{96,64},{128,96},{160,128},{192,160},{224,1... | collective-permute-start | bytes 1572872 | tf_op jit(solution)/shard_map/ppermute | solution.py:221
  93.9 16.2 %collective-permute-start.7 = (bf16[16,128,128]{2,1,0:T(8,128)(2,1)}, bf16[16,128,128]{2,1,0:T(8,128)(2,1)}, u32[]{:S(2)}, u32[]{:S(2)}) collective-permute-start(bf16[16,128,128]{2,1,0:T(8,128)(2,1)} %get-tuple-element.21), channel_id=1, source_target_pairs={{0,32},{32,64},{64,96},{96,128},{128,160},{160,192},{192,224},{224... | collective-permute-start | bytes 1572872 | tf_op jit(solution)/shard_map/ppermute | solution.py:222
  97.1 15.3 %all-to-all-start.2 = ((bf16[16,128,128]{2,1,0:T(8,128)(2,1)}), bf16[16,128,128]{2,1,0:T(8,128)(2,1)}, u32[]{:S(2)}, u32[]{:S(2)}) async-start(bf16[16,128,128]{2,1,0:T(8,128)(2,1)} %copy-done), calls=%async_computation.2 | async-start | bytes 1048576 | tf_op jit(solution)/shard_map/all_to_all | solution.py:196
  112.4 13.7 %all-to-all-start.3 = ((bf16[16,128,128]{2,1,0:T(8,128)(2,1)}), bf16[16,128,128]{2,1,0:T(8,128)(2,1)S(1)}, u32[]{:S(2)}, u32[]{:S(2)}) async-start(bf16[16,128,128]{2,1,0:T(8,128)(2,1)} %fusion.1), calls=%async_computation.3 | async-start | bytes 1048576 | tf_op jit(solution)/shard_map/all_to_all | solution.py:196
  126.1 0.8 copy-start.3

commit v2 on v1

v2 whole, which is shorter than its diff:
```python
import math

import jax
import jax.numpy as jnp
from jax import lax
from jax.experimental import pallas as pl
from jax.experimental.pallas import tpu as pltpu
from jax.sharding import Mesh, PartitionSpec as P

H = 16
E = 64
BLK = 128
NNB = 8
PLANES = 3
PACK_STEPS = 4
LOG2E = 1.4426950408889634

AXES = ("z", "yl", "yh", "x", "core")
HEADS = ("yl", "yh", "x")
VMEM = pltpu.VMEM


def pack_kernel(a_hbm, b_hbm, o_hbm, a_buf, b_buf, o_buf, in_sems, out_sems):
    wide = 2 * E * H // 2 // PACK_STEPS
    tall = H // PACK_STEPS

    def fetch(src, dst, which, i):
        cols = pl.ds(i * wide, wide)
        return pltpu.make_async_copy(src.at[:, cols], dst.at[:, cols], in_sems.at[which, i])

    def put(i):
        rows = pl.ds(i * tall, tall)
        return pltpu.make_async_copy(o_buf.at[rows], o_hbm.at[rows], out_sems.at[i])

    for i in range(PACK_STEPS):
        fetch(a_hbm, a_buf, 0, i).start()
        fetch(b_hbm, b_buf, 1, i).start()
    for i in range(PACK_STEPS):
        fetch(a_hbm, a_buf, 0, i).wait()
        fetch(b_hbm, b_buf, 1, i).wait()
        for pair in range(i * tall // 2, (i + 1) * tall // 2):
            cols = slice(pair * 2 * E, (pair + 1) * 2 * E)
            a = a_buf[:, cols]
            b = b_buf[:, cols]
            o_buf[2 * pair] = jnp.concatenate([a[:, :E], b[:, :E]], axis=1)
            o_buf[2 * pair + 1] = jnp.concatenate([a[:, E:], b[:, E:]], axis=1)
        put(i).start()
    for i in range(PACK_STEPS):
        put(i).wait()


def pack(a, b):
    rows, width = a.shape
    joined = (H, rows, 2 * E)
    return pl.pallas_call(
        pack_kernel,
        out_shape=jax.ShapeDtypeStruct(joined, a.dtype),
        in_specs=[pl.BlockSpec(memory_space=pl.ANY)] * 2,
        out_specs=pl.BlockSpec(memory_space=pl.ANY),
        scratch_shapes=[
            pltpu.VMEM((rows, width), a.dtype),
            pltpu.VMEM((rows, width), a.dtype),
            pltpu.VMEM(joined, a.dtype),
            pltpu.SemaphoreType.DMA((2, PACK_STEPS)),
            pltpu.SemaphoreType.DMA((PACK_STEPS,)),
        ],
        cost_estimate=pl.CostEstimate(flops=0, bytes_accessed=1 << 20, transcendentals=0),
        name="pack",
    )(a, b)


def unpack_kernel(i_ref, a_ref, b_ref):
    for pair in range(H // 2):
        cols = slice(pair * 2 * E, (pair + 1) * 2 * E)
        even = i_ref[2 * pair]
        odd = i_ref[2 * pair + 1]
        a_ref[:, cols] = jnp.concatenate([even[:, :E], odd[:, :E]], axis=1)
        b_ref[:, cols] = jnp.concatenate([even[:, E:], odd[:, E:]], axis=1)


def unpack(joined):
    rows = joined.shape[1]
    shape = jax.ShapeDtypeStruct((rows, H * E), joined.dtype)
    return pl.pallas_call(
        unpack_kernel,
        out_shape=(shape, shape),
        in_specs=[pl.BlockSpec(memory_space=VMEM)],
        out_specs=[pl.BlockSpec(memory_space=VMEM)] * 2,
        compiler_params=pltpu.CompilerParams(vmem_limit_bytes=4 << 20),
        cost_estimate=pl.CostEstimate(flops=0, bytes_accessed=1 << 20, transcendentals=0),
        name="unpack",
    )(joined)


def sides_kernel(own_ref, mine_ref, before_ref, after_ref, here_ref):
    blocks = before_ref.shape[0]

    @pl.loop(0, blocks)
    def _(i):
        before = own_ref[i] + mine_ref[i].astype(jnp.float32)
        after = own_ref[2 * blocks + i] + mine_ref[2 * blocks + i].astype(jnp.float32)
        before_ref[i] = before.astype(before_ref.dtype)
        after_ref[i] = after.astype(after_ref.dtype)
        here_ref[i] = own_ref[blocks + i] + mine_ref[blocks + i].astype(jnp.float32)


def sides(own, mine):
    shape = jax.ShapeDtypeStruct((own.shape[0] // PLANES,) + own.shape[1:], mine.dtype)
    return pl.pallas_call(
        sides_kernel,
        out_shape=(shape, shape, jax.ShapeDtypeStruct(shape.shape, jnp.float32)),
        in_specs=[pl.BlockSpec(memory_space=VMEM)] * 2,
        out_specs=[pl.BlockSpec(memory_space=VMEM)] * 3,
        compiler_params=pltpu.CompilerParams(vmem_limit_bytes=8 << 20),
        cost_estimate=pl.CostEstimate(flops=0, bytes_accessed=4 << 20, transcendentals=0),
        name="sides",
    )(own, mine)


def finish_kernel(here_ref, first_ref, second_ref, o_hbm, o_buf, sems):
    blocks = here_ref.shape[0]
    tall = blocks // PACK_STEPS

    def put(i):
        rows = pl.ds(i * tall, tall)
        return pltpu.make_async_copy(o_buf.at[rows], o_hbm.at[rows], sems.at[i])

    for i in range(PACK_STEPS):
        for j in range(i * tall, (i + 1) * tall):
            total = first_ref[j].astype(jnp.float32) + second_ref[j].astype(jnp.float32)
            total = here_ref[j] + total
            o_buf[j] = total.astype(o_buf.dtype)
        put(i).start()
    for i in range(PACK_STEPS):
        put(i).wait()


def finish(here, first, second):
    return pl.pallas_call(
        finish_kernel,
        out_shape=jax.ShapeDtypeStruct(first.shape, first.dtype),
        in_specs=[pl.BlockSpec(memory_space=VMEM)] * 3,
        out_specs=pl.BlockSpec(memory_space=pl.ANY),
        scratch_shapes=[pltpu.VMEM(first.shape, first.dtype), pltpu.SemaphoreType.DMA((PACK_STEPS,))],
        compiler_params=pltpu.CompilerParams(vmem_limit_bytes=8 << 20),
        cost_estimate=pl.CostEstimate(flops=0, bytes_accessed=3 << 20, transcendentals=0),
        name="finish",
    )(here, first, second)


def attend_group(group, slots, index_of, qg_ref, win, acc, st, oq_ref):
    low = lax.broadcasted_iota(jnp.int32, (BLK, 2 * E), 1) < E
    members = range(len(group))
    both = []
    where = []
    for s, b, used in group:
        qg = qg_ref[s]
        zero = jnp.zeros_like(qg)
        both.append(
            jnp.concatenate(
                [jnp.where(low, qg * jnp.bfloat16(0.125), zero), jnp.where(low, zero, qg)], axis=0
            )
        )
        where.append([index_of(j, b) for j in range(slots)])
    highest = [None for _ in members]
    for j in range(slots):
        for m in members:
            pair = lax.dot_general(
                win[where[m][j]],
                both[m],
                (((1,), (1,)), ((), ())),
                preferred_element_type=jnp.float32,
            )
            scores = pair[:, :BLK]
            if j > 0:
                scores = jnp.where(j < group[m][2], scores, -1e30)
            st[m, j, :, :BLK] = scores
            st[m, j, :, BLK:] = pair[:, BLK:]
            top = jnp.max(scores, axis=0, keepdims=True)
            highest[m] = top if j == 0 else jnp.maximum(highest[m], top)
    total = [jnp.zeros((1, BLK), jnp.float32) for _ in members]
    mixed = [jnp.zeros((1, BLK), jnp.float32) for _ in members]
    for j in range(slots):
        for m in members:
            raised = jnp.exp2((st[m, j, :, :BLK] - highest[m]) * LOG2E)
            st[m, j, :, :BLK] = raised
            total[m] = total[m] + jnp.sum(raised, axis=0, keepdims=True)
            mixed[m] = mixed[m] + jnp.sum(raised * st[m, j, :, BLK:], axis=0, keepdims=True)
    inverse = [1.0 / total[m] for m in members]
    delta = [mixed[m] * inverse[m] for m in members]
    sums = [None for _ in members]
    for j in range(slots):
        for m in members:
            probability = st[m, j, :, :BLK] * inverse[m]
            dscore = probability * (st[m, j, :, BLK:] - delta[m])
            joined = jnp.concatenate(
                [dscore.astype(jnp.bfloat16), probability.astype(jnp.bfloat16)], axis=1
            )
            acc[where[m][j]] += jnp.dot(joined, both[m], preferred_element_type=jnp.float32)
            part = jnp.dot(win[where[m][j]].T, joined, preferred_element_type=jnp.float32)
            sums[m] = part if j == 0 else sums[m] + part
    for m in members:
        result = jnp.concatenate([sums[m][:E, :BLK] * 0.125, sums[m][E:, BLK:]], axis=0)
        oq_ref[group[m][0]] = result.T.astype(oq_ref.dtype)


def attend_kernel(
    place, variants, size, nbr, cnt, qg_ref, *rest
):
    kv_refs = rest[:6]
    oq_ref, own_ref, other_ref = rest[6:9]
    win, acc, st, order, fill, sems = rest[9:]
    z, core = place()
    blocks = qg_ref.shape[0]
    plane_blocks = 2 * blocks
    all_blocks = cnt.shape[0]
    copies = [
        pltpu.make_async_copy(kv_refs[i], win.at[pl.ds(i * blocks, blocks)], sems.at[i])
        for i in range(6)
    ]
    for copy in copies:
        copy.start()
    first = (z - 1) * plane_blocks

    @pl.loop(0, 6 * blocks)
    def _(i):
        acc[i] = jnp.zeros_like(acc[i])

    def block_of(s):
        return z * plane_blocks + 2 * s + core

    for c in range(NNB + 2):
        fill[c] = 0

    @pl.loop(0, blocks)
    def _(s):
        c = cnt[block_of(s)]
        fill[c + 1] += 1

    for c in range(2, NNB + 1):
        fill[c] += fill[c - 1]

    @pl.loop(0, blocks)
    def _(s):
        c = cnt[block_of(s)]
        order[fill[c]] = s
        fill[c] += 1

    for copy in copies:
        copy.wait()

    def index_of(j, b):
        rel = lax.rem(nbr[j, b] - first + all_blocks, all_blocks)
        side = lax.rem(rel + core, 2)
        return side * (PLANES * blocks) + lax.div(rel, 2)

    @pl.loop(0, blocks // size)
    def _(i):
        group = []
        for m in range(size):
            s = order[i * size + m]
            b = block_of(s)
            group.append((s, b, cnt[b]))
        most = group[-1][2]
        before = 0
        for slots in variants:

            @pl.when((most > before) & (most <= slots))
            def _(slots=slots):
                attend_group(group, slots, index_of, qg_ref, win, acc, st, oq_ref)

            before = slots

    @pl.loop(0, PLANES * blocks)
    def _(i):
        own_ref[i] = acc[i]
        other_ref[i] = acc[PLANES * blocks + i].astype(other_ref.dtype)


def attend(place, nbr_t, counts, qg, kvs, variants=(2, 4, 6, 8), size=4):
    import functools

    blocks = qg.shape[0]
    tile = (BLK, 2 * E)
    return pl.pallas_call(
        functools.partial(attend_kernel, place, variants, size),
        out_shape=(
            jax.ShapeDtypeStruct((blocks,) + tile, jnp.bfloat16),
            jax.ShapeDtypeStruct((PLANES * blocks,) + tile, jnp.float32),
            jax.ShapeDtypeStruct((PLANES * blocks,) + tile, jnp.bfloat16),
        ),
        in_specs=[pl.BlockSpec(memory_space=pltpu.SMEM)] * 2
        + [pl.BlockSpec(memory_space=VMEM)]
        + [pl.BlockSpec(memory_space=pltpu.HBM)] * 6,
        out_specs=[pl.BlockSpec(memory_space=VMEM)] * 3,
        scratch_shapes=[
            pltpu.VMEM((6 * blocks,) + tile, jnp.bfloat16),
            pltpu.VMEM((6 * blocks,) + tile, jnp.float32),
            pltpu.VMEM((size, NNB, BLK, 2 * BLK), jnp.float32),
            pltpu.SMEM((blocks,), jnp.int32),
            pltpu.SMEM((NNB + 2,), jnp.int32),
            pltpu.SemaphoreType.DMA((6,)),
        ],
        compiler_params=pltpu.CompilerParams(vmem_limit_bytes=18 << 20),
        cost_estimate=pl.CostEstimate(
            flops=2 * 5 * blocks * 5 * BLK * BLK * E,
            bytes_accessed=8 << 20,
            transcendentals=blocks * 5 * BLK * BLK,
        ),
        name="attend",
    )(nbr_t, counts, qg, *kvs)


def on_device(query, key, value, grad_out, neighbour, counts):
    planes = lax.axis_size("z")
    up = [(i, (i + 1) % planes) for i in range(planes)]
    down = [(i, (i - 1) % planes) for i in range(planes)]
    swap = [(0, 1), (1, 0)]

    def exchange(packed):
        return lax.all_to_all(packed, HEADS, split_axis=0, concat_axis=0, tiled=True)

    kv = exchange(pack(key, value))
    kv, qg_packed = lax.optimization_barrier((kv, pack(query, grad_out)))
    kv_before = lax.ppermute(kv, "z", up)
    kv_after = lax.ppermute(kv, "z", down)
    qg = exchange(qg_packed)
    kv_other = lax.ppermute(kv, "core", swap)
    kv_before, kv_after, qg = lax.optimization_barrier((kv_before, kv_after, qg))
    before_other = lax.ppermute(kv_before, "core", swap)
    after_other = lax.ppermute(kv_after, "core", swap)

    def place():
        return lax.axis_index("z"), lax.axis_index("core")

    oq, own, other = attend(
        place,
        neighbour.T,
        counts,
        qg,
        (kv_before, kv, kv_after, before_other, kv_other, after_other),
    )
    mine = lax.ppermute(other, "core", swap)
    to_before, to_after, here = sides(own, mine)
    from_after = lax.ppermute(to_before, "z", down)
    from_before = lax.ppermute(to_after, "z", up)
    back_oq = exchange(oq)
    total = finish(here, from_after, from_before)
    dquery, out = unpack(back_oq)
    dkey, dvalue = unpack(exchange(total))
    return out, dquery, dkey, dvalue


def solution(mesh):
    inner = Mesh(mesh.devices.reshape(16, 2, 2, 4, 2), AXES)
    return jax.shard_map(
        on_device,
        mesh=inner,
        in_specs=(P(AXES, None),) * 4 + (P(), P()),
        out_specs=(P(AXES, None),) * 4,
        check_vma=False,
    )
```

time: 130 us -> 111 us (0.85)
  blocking collectives: 31.6 us -> 0 us
  waiting for transfers between devices: 24.4 us -> 37.6 us
  starting transfers between devices: 42.9 us -> 51.6 us
  Pallas kernels: 24.5 us -> 19 us
  other arithmetic: 2.87 us -> 0 us
  local copies, waits for them, and re-layouts: 1.9 us -> 0.01 us
    all_to_all x2 -> x0, blocking collectives: 31.6 us -> none  [exchange(): lax.all_to_all(packed, HEADS, split_axis=0, concat_axis=0, tiled=True)]
    all_to_all x2 -> x4, waiting for transfers between devices: 8.18 us -> 22.1 us  [exchange(): lax.all_to_all(packed, HEADS, split_axis=0, concat_axis=0, tiled=True)]
    all_to_all x2 -> x4, starting transfers between devices: 7.83 us -> 18.3 us  [exchange(): lax.all_to_all(packed, HEADS, split_axis=0, concat_axis=0, tiled=True)]
    ppermute x1, waiting for transfers between devices: 3.59 us -> 0.01 us  [on_device(): kv_after = lax.ppermute(kv, 'z', down)]
    pallas_call x3 -> x5, Pallas kernels: 20.5 us -> 17 us  [the longest x1 10.9 us: attend(): pl.pallas_call(functools.partial(attend_kernel, place, variants, size), o...]
    ppermute x1, starting transfers between devices: 4.52 us -> 1.92 us  [on_device(): after_other = lax.ppermute(kv_after, 'core', swap)]
    ppermute x1, starting transfers between devices: 2.01 us -> 4.28 us  [on_device(): from_after = lax.ppermute(to_before, 'z', down)]
    convert_element_type x1 -> x0, other arithmetic: 2.19 us -> none  [on_device(): total = (sums[blocks:2 * blocks] + from_after.astype(jnp.float32) + from_...]
  transfers between devices with their start and end apart: 10 -> 12, of which waited for: 7 -> 7; matrix products, arithmetic and copies ran while one was open for 2% -> 0% of each run, Pallas kernels for 3% -> 4%
where the time goes in v2:
time: 111 us; the launch traced here: 109 us
  starting transfers between devices  51.6 us (46%)
  waiting for transfers between devices  37.6 us (34%)
  Pallas kernels  19 us (17%)
    all_to_all x4, waiting for transfers between devices, exchange(): lax.all_to_all(packed, HEADS, split_axis=0, concat_axis=0, tiled=True)  22.1 us
    all_to_all x4, starting transfers between devices, exchange(): lax.all_to_all(packed, HEADS, split_axis=0, concat_axis=0, tiled=True)  18.3 us
    ppermute x1, starting transfers between devices, on_device(): kv_after = lax.ppermute(kv, 'z', down)  12.6 us
    pallas_call x1, Pallas kernels, attend(): pl.pallas_call(functools.partial(attend_kernel, place, variants, size), o...  10.9 us
    ppermute x1, waiting for transfers between devices, on_device(): from_after = lax.ppermute(to_before, 'z', down)  5.68 us
    ppermute x1, waiting for transfers between devices, on_device(): from_before = lax.ppermute(to_after, 'z', up)  4.73 us
    ppermute x1, starting transfers between devices, on_device(): before_other = lax.ppermute(kv_before, 'core', swap)  4.56 us
    ppermute x1, starting transfers between devices, on_device(): from_after = lax.ppermute(to_before, 'z', down)  4.28 us
  transfers between devices with their start and end apart: 12, of which 7 were waited for; matrix products, arithmetic and copies ran while one was open for 0% of the time, Pallas kernels for 4%

profile of v2, /device:TPU:1, one launch (start us, length us, event | category | flops | bytes accessed | tf_op | source)
XLA Modules:
  0.0 109.0 jit_solution(774832268164665671)
XLA Ops:
  0.6 2.0 %pack.2 = bf16[16,128,128]{2,1,0:T(8,128)(2,1)} custom-call(bf16[128,1024]{1,0:T(8,128)(2,1)} %a_hbm.2, bf16[128,1024]{1,0:T(8,128)(2,1)} %b_hbm.2), custom_call_target="tpu_custom_call" | custom-call | bytes 1048576 | tf_op jit(solution)/shard_map/pack/pallas_call | solution.py:55
  2.7 0.0 copy-start
  2.7 0.0 copy-start.1
  2.7 7.6 %all-to-all-start = ((bf16[16,128,128]{2,1,0:T(8,128)(2,1)}), bf16[16,128,128]{2,1,0:T(8,128)(2,1)S(1)}, u32[]{:S(2)}, u32[]{:S(2)}) async-start(bf16[16,128,128]{2,1,0:T(8,128)(2,1)} %pack.2), calls=%async_computation | async-start | bytes 1048576 | tf_op jit(solution)/shard_map/all_to_all | solution.py:321
  10.3 2.0 %pack.3 = bf16[16,128,128]{2,1,0:T(8,128)(2,1)} custom-call(bf16[128,1024]{1,0:T(8,128)(2,1)} %a_hbm.3, bf16[128,1024]{1,0:T(8,128)(2,1)} %b_hbm.3), custom_call_target="tpu_custom_call" | custom-call | bytes 1048576 | tf_op jit(solution)/shard_map/pack/pallas_call | solution.py:55
  12.4 7.1 %all-to-all-done.rest_1_ = bf16[16,128,128]{2,1,0:T(8,128)(2,1)S(1)} async-done(((bf16[16,128,128]{2,1,0:T(8,128)(2,1)}), bf16[16,128,128]{2,1,0:T(8,128)(2,1)S(1)}, u32[]{:S(2)}, u32[]{:S(2)}) %all-to-all-start) | async-done | bytes 524320 | tf_op jit(solution)/shard_map/all_to_all | solution.py:321
  19.5 12.6 %collective-permute-start.1 = (bf16[16,128,128]{2,1,0:T(8,128)(2,1)S(1)}, bf16[16,128,128]{2,1,0:T(8,128)(2,1)S(1)}, u32[]{:S(2)}, u32[]{:S(2)}) collective-permute-start(bf16[16,128,128]{2,1,0:T(8,128)(2,1)S(1)} %all-to-all-done.rest_1_), channel_id=1, source_target_pairs={{0,480},{32,0},{64,32},{96,64},{128,96},{160,128},{192,160},{224,1... | collective-permute-start | bytes 1572872 | tf_op jit(solution)/shard_map/ppermute | solution.py:326
  32.1 1.9 %collective-permute-start = (bf16[16,128,128]{2,1,0:T(8,128)(2,1)S(1)}, bf16[16,128,128]{2,1,0:T(8,128)(2,1)S(1)}, u32[]{:S(2)}, u32[]{:S(2)}) collective-permute-start(bf16[16,128,128]{2,1,0:T(8,128)(2,1)S(1)} %all-to-all-done.rest_1_), channel_id=1, source_target_pairs={{0,32},{32,64},{64,96},{96,128},{128,160},{160,192},{192,224},{224... | collective-permute-start | bytes 1572872 | tf_op jit(solution)/shard_map/ppermute | solution.py:325
  34.1 3.6 %all-to-all-start.1 = ((bf16[16,128,128]{2,1,0:T(8,128)(2,1)}), bf16[16,128,128]{2,1,0:T(8,128)(2,1)S(1)}, u32[]{:S(2)}, u32[]{:S(2)}) async-start(bf16[16,128,128]{2,1,0:T(8,128)(2,1)} %pack.3), calls=%async_computation.1 | async-start | bytes 1048576 | tf_op jit(solution)/shard_map/all_to_all | solution.py:321
  37.7 4.0 %collective-permute-start.3 = (bf16[16,128,128]{2,1,0:T(8,128)(2,1)S(1)}, bf16[16,128,128]{2,1,0:T(8,128)(2,1)S(1)}, u32[]{:S(2)}, u32[]{:S(2)}) collective-permute-start(bf16[16,128,128]{2,1,0:T(8,128)(2,1)S(1)} %all-to-all-done.rest_1_), channel_id=1, source_target_pairs={{0,1},{1,0},{2,3},{3,2},{4,5},{5,4},{6,7},{7,6},{8,9},{9,8},{10,11... | collective-permute-start | bytes 1572872 | tf_op jit(solution)/shard_map/ppermute | solution.py:328
  41.6 5.9 %all-to-all-done.1.qg_ref = bf16[16,128,128]{2,1,0:T(8,128)(2,1)S(1)} async-done(((bf16[16,128,128]{2,1,0:T(8,128)(2,1)}), bf16[16,128,128]{2,1,0:T(8,128)(2,1)S(1)}, u32[]{:S(2)}, u32[]{:S(2)}) %all-to-all-start.1) | async-done | bytes 524320 | tf_op jit(solution)/shard_map/all_to_all | solution.py:321
  47.5 0.0 collective-permute-done.1.rest_2_
  47.5 0.0 collective-permute-done.rest_0_
  47.5 4.6 %collective-permute-start.2 = (bf16[16,128,128]{2,1,0:T(8,128)(2,1)S(1)}, bf16[16,128,128]{2,1,0:T(8,128)(2,1)S(1)}, u32[]{:S(2)}, u32[]{:S(2)}) collective-permute-start(bf16[16,128,128]{2,1,0:T(8,128)(2,1)S(1)} %collective-permute-done.rest_0_), channel_id=1, source_target_pairs={{0,1},{1,0},{2,3},{3,2},{4,5},{5,4},{6,7},{7,6},{8,9},{9,8},{10,11... | collective-permute-start | bytes 1572872 | tf_op jit(solution)/shard_map/ppermute | solution.py:330
  52.1 1.9 %collective-permute-start.4 = (bf16[16,128,128]{2,1,0:T(8,128)(2,1)S(1)}, bf16[16,128,128]{2,1,0:T(8,128)(2,1)S(1)}, u32[]{:S(2)}, u32[]{:S(2)}) collective-permute-start(bf16[16,128,128]{2,1,0:T(8,128)(2,1)S(1)} %collective-permute-done.1.rest_2_), channel_id=1, source_target_pairs={{0,1},{1,0},{2,3},{3,2},{4,5},{5,4},{6,7},{7,6},{8,9},{9,8},{10,11... | collective-permute-start | bytes 1572872 | tf_op jit(solution)/shard_map/ppermute | solution.py:331
  54.0 0.0 collective-permute-done.3.rest_4_
  54.0 0.0 collective-permute-done.2.rest_3_
  54.0 1.9 %collective-permute-done.4.rest_5_ = bf16[16,128,128]{2,1,0:T(8,128)(2,1)S(1)} collective-permute-done((bf16[16,128,128]{2,1,0:T(8,128)(2,1)S(1)}, bf16[16,128,128]{2,1,0:T(8,128)(2,1)S(1)}, u32[]{:S(2)}, u32[]{:S(2)}) %collective-permute-start.4) | collective-permute-done | bytes 524320 | tf_op jit(solution)/shard_map/ppermute | solution.py:331
  55.9 10.9 %attend.1 = (bf16[16,128,128]{2,1,0:T(8,128)(2,1)}, f32[48,128,128]{2,1,0:T(8,128)S(1)}, bf16[48,128,128]{2,1,0:T(8,128)(2,1)S(1)}) custom-call(s32[8,512]{1,0:T(8,128)S(1)} %bitcast.1, s32[512]{0:T(512)S(1)} %copy-done.1, bf16[16,128,128]{2,1,0:T(8,128)(2,1)S(1)} %all-to-all-done.1.qg_ref, bf16[16,128,128]{2,1,0:T(8,128)(2,1)S(1)} %collective-permute-done.rest_0_, ...), custom_call_target="tpu_custom_call" | custom-call | flops 838860800 | bytes 8388608 | tf_op jit(solution)/shard_map/attend/pallas_call | solution.py:285
  66.8 2.1 %collective-permute-start.5 = (bf16[48,128,128]{2,1,0:T(8,128)(2,1)S(1)}, bf16[48,128,128]{2,1,0:T(8,128)(2,1)S(1)}, u32[]{:S(2)}, u32[]{:S(2)}) collective-permute-start(bf16[48,128,128]{2,1,0:T(8,128)(2,1)S(1)} %get-tuple-element.28), channel_id=1, source_target_pairs={{0,1},{1,0},{2,3},{3,2},{4,5},{5,4},{6,7},{7,6},{8,9},{9,8},{10,11... | collective-permute-start | bytes 4718600 | tf_op jit(solution)/shard_map/ppermute | solution.py:343
  68.9 3.2 %collective-permute-done.5.mine_ref = bf16[48,128,128]{2,1,0:T(8,128)(2,1)S(1)} collective-permute-done((bf16[48,128,128]{2,1,0:T(8,128)(2,1)S(1)}, bf16[48,128,128]{2,1,0:T(8,128)(2,1)S(1)}, u32[]{:S(2)}, u32[]{:S(2)}) %collective-permute-start.5) | collective-permute-done | bytes 1572896 | tf_op jit(solution)/shard_map/ppermute | solution.py:343
  72.1 1.1 %sides.1 = (bf16[16,128,128]{2,1,0:T(8,128)(2,1)}, bf16[16,128,128]{2,1,0:T(8,128)(2,1)S(1)}, f32[16,128,128]{2,1,0:T(8,128)S(1)}) custom-call(f32[48,128,128]{2,1,0:T(8,128)S(1)} %get-tuple-element.27.own_ref, bf16[48,128,128]{2,1,0:T(8,128)(2,1)S(1)} %collective-permute-done.5.mine_ref), custom_call_target="tpu_custom_call" | custom-call | bytes 4194304 | tf_op jit(solution)/shard_map/sides/pallas_call | solution.py:109
  73.2 4.3 %collective-permute-start.6 = (bf16[16,128,128]{2,1,0:T(8,128)(2,1)}, bf16[16,128,128]{2,1,0:T(8,128)(2,1)S(1)}, u32[]{:S(2)}, u32[]{:S(2)}) collective-permute-start(bf16[16,128,128]{2,1,0:T(8,128)(2,1)} %get-tuple-element.30), channel_id=1, source_target_pairs={{0,480},{32,0},{64,32},{96,64},{128,96},{160,128},{192,160},{224,1... | collective-permute-start | bytes 1572872 | tf_op jit(solution)/shard_map/ppermute | solution.py:345
  77.5 1.9 %collective-permute-start.7 = (bf16[16,128,128]{2,1,0:T(8,128)(2,1)S(1)}, bf16[16,128,128]{2,1,0:T(8,128)(2,1)S(1)}, u32[]{:S(2)}, u32[]{:S(2)}) collective-permute-start(bf16[16,128,128]{2,1,0:T(8,128)(2,1)S(1)} %get-tuple-element.31), channel_id=1, source_target_pairs={{0,32},{32,64},{64,96},{96,128},{128,160},{160,192},{192,224},{224... | collective-permute-start | bytes 1572872 | tf_op jit(solution)/shard_map/ppermute | solution.py:346
  79.4 3.6 %all-to-all-start.2 = ((bf16[16,128,128]{2,1,0:T(8,128)(2,1)}), bf16[16,128,128]{2,1,0:T(8,128)(2,1)S(1)}, u32[]{:S(2)}, u32[]{:S(2)}) async-start(bf16[16,128,128]{2,1,0:T(8,128)(2,1)} %get-tuple-element.24), calls=%async_computation.2 | async-start | bytes 1048576 | tf_op jit(solution)/shard_map/all_to_all | solution.py:321
  83.0 5.7 %collective-permute-done.6.first_ref = bf16[16,128,128]{2,1,0:T(8,128)(2,1)S(1)} collective-permute-done((bf16[16,128,128]{2,1,0:T(8,128)(2,1)}, bf16[16,128,128]{2,1,0:T(8,128)(2,1)S(1)}, u32[]{:S(2)}, u32[]{:S(2)}) %collective-permute-start.6) | collective-permute-done | bytes 524320 | tf_op jit(solution)/shard_map/ppermute | solution.py:345
  88.7 4.7 %collective-permute-done.7.second_ref = bf16[16,128,128]{2,1,0:T(8,128)(2,1)S(1)} collective-permute-done((bf16[16,128,128]{2,1,0:T(8,128)(2,1)S(1)}, bf16[16,128,128]{2,1,0:T(8,128)(2,1)S(1)}, u32[]{:S(2)}, u32[]{:S(2)}) %collective-permute-start.7) | collective-permute-done | bytes 524320 | tf_op jit(solution)/shard_map/ppermute | solution.py:346
  93.4 0.9 finish.1
  94.3 3.6 %all-to-all-start.3 = ((bf16[16,128,128]{2,1,0:T(8,128)(2,1)}), bf16[16,128,128]{2,1,0:T(8,128)(2,1)S(1)}, u32[]{:S(2)}, u32[]{:S(2)}) async-start(bf16[16,128,128]{2,1,0:T(8,128)(2,1)} %finish.1), calls=%async_computation.3 | async-start | bytes 1048576 | tf_op jit(solution)/shard_map/all_to_all | solution.py:321
  97.9 1.0 unpack.2
  98.9 9.1 %all-to-all-done.3.i_ref = bf16[16,128,128]{2,1,0:T(8,128)(2,1)S(1)} async-done(((bf16[16,128,128]{2,1,0:T(8,128)(2,1)}), bf16[16,128,128]{2,1,0:T(8,128)(2,1)S(1)}, u32[]{:S(2)}, u32[]{:S(2)}) %all-to-all-start.3) | async-done | bytes 524320 | tf_op jit(solution)/shard_map/all_to_all | solution.py:321
  108.0 1.0 unpack.3
  (3 shorter events, 0.0 us)
Async XLA Ops:
  2.7 53.2 %copy-start = (s32[512,8]{0,1:T(8,128)S(1)}, s32[512,8]{0,1:T(8,128)}, u32[]{:S(2)}) copy-start(s32[512,8]{0,1:T(8,128)} %param.10) | copy-start | bytes 49156
  2.7 53.2 %copy-start.1 = (s32[512]{0:T(512)S(1)}, s32[512]{0:T(512)}, u32[]{:S(2)}) copy-start(s32[512]{0:T(512)} %cnt.1) | copy-start | bytes 6148
  2.7 16.8 %all-to-all-start = ((bf16[16,128,128]{2,1,0:T(8,128)(2,1)}), bf16[16,128,128]{2,1,0:T(8,128)(2,1)S(1)}, u32[]{:S(2)}, u32[]{:S(2)}) async-start(bf16[16,128,128]{2,1,0:T(8,128)(2,1)} %pack.2), calls=%async_computation | async-start | bytes 1048576 | tf_op jit(solution)/shard_map/all_to_all | solution.py:321
  19.5 28.0 %collective-permute-start.1 = (bf16[16,128,128]{2,1,0:T(8,128)(2,1)S(1)}, bf16[16,128,128]{2,1,0:T(8,128)(2,1)S(1)}, u32[]{:S(2)}, u32[]{:S(2)}) collective-permute-start(bf16[16,128,128]{2,1,0:T(8,128)(2,1)S(1)} %all-to-all-done.rest_1_), channel_id=1, source_target_pairs={{0,480},{32,0},{64,32},{96,64},{128,96},{160,128},{192,160},{224,1... | collective-permute-start | bytes 1572872 | tf_op jit(solution)/shard_map/ppermute | solution.py:326
  32.1 15.4 %collective-permute-start = (bf16[16,128,128]{2,1,0:T(8,128)(2,1)S(1)}, bf16[16,128,128]{2,1,0:T(8,128)(2,1)S(1)}, u32[]{:S(2)}, u32[]{:S(2)}) collective-permute-start(bf16[16,128,128]{2,1,0:T(8,128)(2,1)S(1)} %all-to-all-done.rest_1_), channel_id=1, source_target_pairs={{0,32},{32,64},{64,96},{96,128},{128,160},{160,192},{192,224},{224... | collective-permute-start | bytes 1572872 | tf_op jit(solution)/shard_map/ppermute | solution.py:325
  34.1 13.4 %all-to-all-start.1 = ((bf16[16,128,128]{2,1,0:T(8,128)(2,1)}), bf16[16,128,128]{2,1,0:T(8,128)(2,1)S(1)}, u32[]{:S(2)}, u32[]{:S(2)}) async-start(bf16[16,128,128]{2,1,0:T(8,128)(2,1)} %pack.3), calls=%async_computation.1 | async-start | bytes 1048576 | tf_op jit(solution)/shard_map/all_to_all | solution.py:321
  37.7 16.3 %collective-permute-start.3 = (bf16[16,128,128]{2,1,0:T(8,128)(2,1)S(1)}, bf16[16,128,128]{2,1,0:T(8,128)(2,1)S(1)}, u32[]{:S(2)}, u32[]{:S(2)}) collective-permute-start(bf16[16,128,128]{2,1,0:T(8,128)(2,1)S(1)} %all-to-all-done.rest_1_), channel_id=1, source_target_pairs={{0,1},{1,0},{2,3},{3,2},{4,5},{5,4},{6,7},{7,6},{8,9},{9,8},{10,11... | collective-permute-start | bytes 1572872 | tf_op jit(solution)/shard_map/ppermute | solution.py:328
  47.5 6.5 %collective-permute-start.2 = (bf16[16,128,128]{2,1,0:T(8,128)(2,1)S(1)}, bf16[16,128,128]{2,1,0:T(8,128)(2,1)S(1)}, u32[]{:S(2)}, u32[]{:S(2)}) collective-permute-start(bf16[16,128,128]{2,1,0:T(8,128)(2,1)S(1)} %collective-permute-done.rest_0_), channel_id=1, source_target_pairs={{0,1},{1,0},{2,3},{3,2},{4,5},{5,4},{6,7},{7,6},{8,9},{9,8},{10,11... | collective-permute-start | bytes 1572872 | tf_op jit(solution)/shard_map/ppermute | solution.py:330
  52.1 3.8 %collective-permute-start.4 = (bf16[16,128,128]{2,1,0:T(8,128)(2,1)S(1)}, bf16[16,128,128]{2,1,0:T(8,128)(2,1)S(1)}, u32[]{:S(2)}, u32[]{:S(2)}) collective-permute-start(bf16[16,128,128]{2,1,0:T(8,128)(2,1)S(1)} %collective-permute-done.1.rest_2_), channel_id=1, source_target_pairs={{0,1},{1,0},{2,3},{3,2},{4,5},{5,4},{6,7},{7,6},{8,9},{9,8},{10,11... | collective-permute-start | bytes 1572872 | tf_op jit(solution)/shard_map/ppermute | solution.py:331
  66.8 5.3 %collective-permute-start.5 = (bf16[48,128,128]{2,1,0:T(8,128)(2,1)S(1)}, bf16[48,128,128]{2,1,0:T(8,128)(2,1)S(1)}, u32[]{:S(2)}, u32[]{:S(2)}) collective-permute-start(bf16[48,128,128]{2,1,0:T(8,128)(2,1)S(1)} %get-tuple-element.28), channel_id=1, source_target_pairs={{0,1},{1,0},{2,3},{3,2},{4,5},{5,4},{6,7},{7,6},{8,9},{9,8},{10,11... | collective-permute-start | bytes 4718600 | tf_op jit(solution)/shard_map/ppermute | solution.py:343
  73.2 15.5 %collective-permute-start.6 = (bf16[16,128,128]{2,1,0:T(8,128)(2,1)}, bf16[16,128,128]{2,1,0:T(8,128)(2,1)S(1)}, u32[]{:S(2)}, u32[]{:S(2)}) collective-permute-start(bf16[16,128,128]{2,1,0:T(8,128)(2,1)} %get-tuple-element.30), channel_id=1, source_target_pairs={{0,480},{32,0},{64,32},{96,64},{128,96},{160,128},{192,160},{224,1... | collective-permute-start | bytes 1572872 | tf_op jit(solution)/shard_map/ppermute | solution.py:345
  77.5 15.9 %collective-permute-start.7 = (bf16[16,128,128]{2,1,0:T(8,128)(2,1)S(1)}, bf16[16,128,128]{2,1,0:T(8,128)(2,1)S(1)}, u32[]{:S(2)}, u32[]{:S(2)}) collective-permute-start(bf16[16,128,128]{2,1,0:T(8,128)(2,1)S(1)} %get-tuple-element.31), channel_id=1, source_target_pairs={{0,32},{32,64},{64,96},{96,128},{128,160},{160,192},{192,224},{224... | collective-permute-start | bytes 1572872 | tf_op jit(solution)/shard_map/ppermute | solution.py:346
  79.4 14.9 %all-to-all-start.2 = ((bf16[16,128,128]{2,1,0:T(8,128)(2,1)}), bf16[16,128,128]{2,1,0:T(8,128)(2,1)S(1)}, u32[]{:S(2)}, u32[]{:S(2)}) async-start(bf16[16,128,128]{2,1,0:T(8,128)(2,1)} %get-tuple-element.24), calls=%async_computation.2 | async-start | bytes 1048576 | tf_op jit(solution)/shard_map/all_to_all | solution.py:321
  94.3 13.7 %all-to-all-start.3 = ((bf16[16,128,128]{2,1,0:T(8,128)(2,1)}), bf16[16,128,128]{2,1,0:T(8,128)(2,1)S(1)}, u32[]{:S(2)}, u32[]{:S(2)}) async-start(bf16[16,128,128]{2,1,0:T(8,128)(2,1)} %finish.1), calls=%async_computation.3 | async-start | bytes 1048576 | tf_op jit(solution)/shard_map/all_to_all | solution.py:321

commit v3 on v2

--- a/solution.py
+++ b/solution.py
@@ -1,4 +1,4 @@
-import math
+import functools
 
 import jax
 import jax.numpy as jnp
@@ -148,12 +148,82 @@
     )(here, first, second)
 
 
-def attend_group(group, slots, index_of, qg_ref, win, acc, st, oq_ref):
+def plan_kernel(place, nbr, cnt, plan, fill):
+    z, core = place()
+    blocks = plan.shape[0]
+    plane_blocks = 2 * blocks
+    all_blocks = cnt.shape[0]
+    first = (z - 1) * plane_blocks
+
+    def block_of(s):
+        return z * plane_blocks + 2 * s + core
+
+    for c in range(NNB + 2):
+        fill[c] = 0
+
+    @pl.loop(0, blocks)
+    def _(s):
+        c = cnt[block_of(s)]
+        fill[c + 1] += 1
+
+    for c in range(2, NNB + 1):
+        fill[c] += fill[c - 1]
+
+    @pl.loop(0, blocks)
+    def _(s):
+        b = block_of(s)
+        c = cnt[b]
+        at = fill[c]
+        fill[c] += 1
+        plan[at, NNB] = s
+        plan[at, NNB + 1] = c
+        for j in range(NNB):
+            rel = lax.rem(nbr[j, b] - first + all_blocks, all_blocks)
+            side = lax.rem(rel + core, 2)
+            plane = lax.div(rel, plane_blocks)
+            slot = jnp.where(lax.rem(rel, 2) == 1, PLANES - 1 - plane, plane)
+            plan[at, j] = (side * PLANES + slot) * blocks + lax.div(
+                lax.rem(rel, plane_blocks), 2
+            )
+
+
+def plan_blocks(place, nbr_t, counts, blocks):
+    return pl.pallas_call(
+        functools.partial(plan_kernel, place),
+        out_shape=jax.ShapeDtypeStruct((blocks, 2 * NNB), jnp.int32),
+        in_specs=[pl.BlockSpec(memory_space=pltpu.SMEM)] * 2,
+        out_specs=pl.BlockSpec(memory_space=pltpu.SMEM),
+        scratch_shapes=[pltpu.SMEM((NNB + 2,), jnp.int32)],
+        compiler_params=pltpu.CompilerParams(vmem_limit_bytes=1 << 20),
+        cost_estimate=pl.CostEstimate(flops=0, bytes_accessed=1 << 20, transcendentals=0),
+        name="plan",
+    )(nbr_t, counts)
+
+
+def join_kernel(a_ref, b_ref, o_ref):
+    blocks = a_ref.shape[0]
+    o_ref[:blocks] = a_ref[...]
+    o_ref[blocks:] = b_ref[...]
+
+
+def join(a, b):
+    return pl.pallas_call(
+        join_kernel,
+        out_shape=jax.ShapeDtypeStruct((2 * a.shape[0],) + a.shape[1:], a.dtype),
+        in_specs=[pl.BlockSpec(memory_space=VMEM)] * 2,
+        out_specs=pl.BlockSpec(memory_space=VMEM),
+        compiler_params=pltpu.CompilerParams(vmem_limit_bytes=4 << 20),
+        cost_estimate=pl.CostEstimate(flops=0, bytes_accessed=2 << 20, transcendentals=0),
+        name="join",
+    )(a, b)
+
+
+def attend_group(group, slots, qg_ref, win, acc, st, jn, oq_ref):
     low = lax.broadcasted_iota(jnp.int32, (BLK, 2 * E), 1) < E
     members = range(len(group))
     both = []
     where = []
-    for s, b, used in group:
+    for s, used, found in group:
         qg = qg_ref[s]
         zero = jnp.zeros_like(qg)
         both.append(
@@ -161,113 +231,94 @@
                 [jnp.where(low, qg * jnp.bfloat16(0.125), zero), jnp.where(low, zero, qg)], axis=0
             )
         )
-        where.append([index_of(j, b) for j in range(slots)])
-    highest = [None for _ in members]
-    for j in range(slots):
-        for m in members:
-            pair = lax.dot_general(
-                win[where[m][j]],
-                both[m],
-                (((1,), (1,)), ((), ())),
-                preferred_element_type=jnp.float32,
-            )
-            scores = pair[:, :BLK]
-            if j > 0:
-                scores = jnp.where(j < group[m][2], scores, -1e30)
-            st[m, j, :, :BLK] = scores
-            st[m, j, :, BLK:] = pair[:, BLK:]
-            top = jnp.max(scores, axis=0, keepdims=True)
-            highest[m] = top if j == 0 else jnp.maximum(highest[m], top)
-    total = [jnp.zeros((1, BLK), jnp.float32) for _ in members]
-    mixed = [jnp.zeros((1, BLK), jnp.float32) for _ in members]
-    for j in range(slots):
-        for m in members:
-            raised = jnp.exp2((st[m, j, :, :BLK] - highest[m]) * LOG2E)
-            st[m, j, :, :BLK] = raised
-            total[m] = total[m] + jnp.sum(raised, axis=0, keepdims=True)
-            mixed[m] = mixed[m] + jnp.sum(raised * st[m, j, :, BLK:], axis=0, keepdims=True)
-    inverse = [1.0 / total[m] for m in members]
-    delta = [mixed[m] * inverse[m] for m in members]
-    sums = [None for _ in members]
-    for j in range(slots):
-        for m in members:
-            probability = st[m, j, :, :BLK] * inverse[m]
-            dscore = probability * (st[m, j, :, BLK:] - delta[m])
-            joined = jnp.concatenate(
-                [dscore.astype(jnp.bfloat16), probability.astype(jnp.bfloat16)], axis=1
-            )
-            acc[where[m][j]] += jnp.dot(joined, both[m], preferred_element_type=jnp.float32)
-            part = jnp.dot(win[where[m][j]].T, joined, preferred_element_type=jnp.float32)
-            sums[m] = part if j == 0 else sums[m] + part
+        where.append([found(j) for j in range(slots)])
+    rows = [slice(j * BLK, (j + 1) * BLK) for j in range(slots)]
+    everything = slice(0, slots * BLK)
+    live = [[j == 0 or j < used for j in range(slots)] for _, used, _ in group]
+    tops = []
     for m in members:
-        result = jnp.concatenate([sums[m][:E, :BLK] * 0.125, sums[m][E:, BLK:]], axis=0)
+        keys = jnp.concatenate([win[where[m][j]] for j in range(slots)], axis=0)
+        st[m, everything] = lax.dot_general(
+            keys, both[m], (((1,), (1,)), ((), ())), preferred_element_type=jnp.float32
+        )
+        top = [jnp.max(st[m, rows[j], :BLK], axis=0, keepdims=True) for j in range(slots)]
+        highest = top[0]
+        for j in range(1, slots):
+            highest = jnp.maximum(highest, jnp.where(live[m][j], top[j], -1e30))
+        tops.append(
+            [highest if j == 0 else jnp.where(live[m][j], highest, 1e30) for j in range(slots)]
+        )
+    inverse = []
+    delta = []
+    for m in members:
+        total = jnp.zeros((1, BLK), jnp.float32)
+        mixed = jnp.zeros((1, BLK), jnp.float32)
+        for j in range(slots):
+            raised = jnp.exp2((st[m, rows[j], :BLK] - tops[m][j]) * LOG2E)
+            st[m, rows[j], :BLK] = raised
+            total = total + jnp.sum(raised, axis=0, keepdims=True)
+            mixed = mixed + jnp.sum(raised * st[m, rows[j], BLK:], axis=0, keepdims=True)
+        inverse.append(1.0 / total)
+        delta.append(mixed * inverse[m])
+    for m in members:
+        for j in range(slots):
+            probability = st[m, rows[j], :BLK] * inverse[m]
+            dscore = probability * (st[m, rows[j], BLK:] - delta[m])
+            jn[m, rows[j], :BLK] = dscore.astype(jnp.bfloat16)
+            jn[m, rows[j], BLK:] = probability.astype(jnp.bfloat16)
+        joined = jn[m, everything]
+        parts = jnp.dot(joined, both[m], preferred_element_type=jnp.float32)
+        for j in range(slots):
+            acc[where[m][j]] += parts[rows[j]]
+        turned = jnp.concatenate([win[where[m][j]].T for j in range(slots)], axis=1)
+        sums = jnp.dot(turned, joined, preferred_element_type=jnp.float32)
+        result = jnp.concatenate([sums[:E, :BLK] * 0.125, sums[E:, BLK:]], axis=0)
         oq_ref[group[m][0]] = result.T.astype(oq_ref.dtype)
 
 
-def attend_kernel(
-    place, variants, size, nbr, cnt, qg_ref, *rest
-):
-    kv_refs = rest[:6]
-    oq_ref, own_ref, other_ref = rest[6:9]
-    win, acc, st, order, fill, sems = rest[9:]
-    z, core = place()
+def entry(plan, at, j):
+    return plan[at, j]
+
+
+def attend_kernel(variants, size, plan, qg_ref, *rest):
+    kv_refs = rest[:4]
+    oq_ref, own_ref, other_ref = rest[4:7]
+    win, acc, st, jn, sems = rest[7:]
     blocks = qg_ref.shape[0]
-    plane_blocks = 2 * blocks
-    all_blocks = cnt.shape[0]
+    pieces = (
+        (1, 0, 0), (0, 0, 1), (2, 1, 1), (4, 0, 2), (3, 0, 3), (5, 1, 3)
+    )
     copies = [
-        pltpu.make_async_copy(kv_refs[i], win.at[pl.ds(i * blocks, blocks)], sems.at[i])
-        for i in range(6)
+        pltpu.make_async_copy(
+            kv_refs[which].at[pl.ds(part * blocks, blocks)],
+            win.at[pl.ds(slot * blocks, blocks)],
+            sems.at[slot],
+        )
+        for slot, part, which in pieces
     ]
     for copy in copies:
         copy.start()
-    first = (z - 1) * plane_blocks
-
-    @pl.loop(0, 6 * blocks)
+
+    @pl.loop(0, 2 * PLANES * blocks)
     def _(i):
         acc[i] = jnp.zeros_like(acc[i])
 
-    def block_of(s):
-        return z * plane_blocks + 2 * s + core
-
-    for c in range(NNB + 2):
-        fill[c] = 0
-
-    @pl.loop(0, blocks)
-    def _(s):
-        c = cnt[block_of(s)]
-        fill[c + 1] += 1
-
-    for c in range(2, NNB + 1):
-        fill[c] += fill[c - 1]
-
-    @pl.loop(0, blocks)
-    def _(s):
-        c = cnt[block_of(s)]
-        order[fill[c]] = s
-        fill[c] += 1
-
     for copy in copies:
         copy.wait()
-
-    def index_of(j, b):
-        rel = lax.rem(nbr[j, b] - first + all_blocks, all_blocks)
-        side = lax.rem(rel + core, 2)
-        return side * (PLANES * blocks) + lax.div(rel, 2)
 
     @pl.loop(0, blocks // size)
     def _(i):
         group = []
         for m in range(size):
-            s = order[i * size + m]
-            b = block_of(s)
-            group.append((s, b, cnt[b]))
-        most = group[-1][2]
+            at = i * size + m
+            group.append((plan[at, NNB], plan[at, NNB + 1], functools.partial(entry, plan, at)))
+        most = group[-1][1]
         before = 0
         for slots in variants:
 
             @pl.when((most > before) & (most <= slots))
             def _(slots=slots):
-                attend_group(group, slots, index_of, qg_ref, win, acc, st, oq_ref)
+                attend_group(group, slots, qg_ref, win, acc, st, jn, oq_ref)
 
             before = slots
 
@@ -277,75 +328,73 @@
         other_ref[i] = acc[PLANES * blocks + i].astype(other_ref.dtype)
 
 
-def attend(place, nbr_t, counts, qg, kvs, variants=(2, 4, 6, 8), size=4):
-    import functools
-
+def attend(plan, qg, kvs, variants=(1, 2, 3, 4, 5, 6, 7, 8), size=4):
     blocks = qg.shape[0]
     tile = (BLK, 2 * E)
     return pl.pallas_call(
-        functools.partial(attend_kernel, place, variants, size),
+        functools.partial(attend_kernel, variants, size),
         out_shape=(
             jax.ShapeDtypeStruct((blocks,) + tile, jnp.bfloat16),
             jax.ShapeDtypeStruct((PLANES * blocks,) + tile, jnp.float32),
             jax.ShapeDtypeStruct((PLANES * blocks,) + tile, jnp.bfloat16),
         ),
-        in_specs=[pl.BlockSpec(memory_space=pltpu.SMEM)] * 2
-        + [pl.BlockSpec(memory_space=VMEM)]
-        + [pl.BlockSpec(memory_space=pltpu.HBM)] * 6,
+        in_specs=[pl.BlockSpec(memory_space=pltpu.SMEM), pl.BlockSpec(memory_space=VMEM)]
+        + [pl.BlockSpec(memory_space=pltpu.HBM)] * 4,
         out_specs=[pl.BlockSpec(memory_space=VMEM)] * 3,
         scratch_shapes=[
             pltpu.VMEM((6 * blocks,) + tile, jnp.bfloat16),
             pltpu.VMEM((6 * blocks,) + tile, jnp.float32),
-            pltpu.VMEM((size, NNB, BLK, 2 * BLK), jnp.float32),
-            pltpu.SMEM((blocks,), jnp.int32),
-            pltpu.SMEM((NNB + 2,), jnp.int32),
+            pltpu.VMEM((size, NNB * BLK, 2 * BLK), jnp.float32),
+            pltpu.VMEM((size, NNB * BLK, 2 * BLK), jnp.bfloat16),
             pltpu.SemaphoreType.DMA((6,)),
         ],
-        compiler_params=pltpu.CompilerParams(vmem_limit_bytes=18 << 20),
+        compiler_params=pltpu.CompilerParams(vmem_limit_bytes=32 << 20),
         cost_estimate=pl.CostEstimate(
             flops=2 * 5 * blocks * 5 * BLK * BLK * E,
             bytes_accessed=8 << 20,
             transcendentals=blocks * 5 * BLK * BLK,
         ),
         name="attend",
-    )(nbr_t, counts, qg, *kvs)
+    )(plan, qg, *kvs)
 
 
 def on_device(query, key, value, grad_out, neighbour, counts):
     planes = lax.axis_size("z")
-    up = [(i, (i + 1) % planes) for i in range(planes)]
-    down = [(i, (i - 1) % planes) for i in range(planes)]
+    out_pairs = []
+    in_pairs = []
+    for i in range(planes):
+        for core in range(2):
+            ahead = (i + 1 - 2 * core) % planes
+            out_pairs.append((2 * i + core, 2 * ahead + core))
+            in_pairs.append((2 * ahead + core, 2 * i + core))
     swap = [(0, 1), (1, 0)]
+
+    def place():
+        return lax.axis_index("z"), lax.axis_index("core")
 
     def exchange(packed):
         return lax.all_to_all(packed, HEADS, split_axis=0, concat_axis=0, tiled=True)
 
     kv = exchange(pack(key, value))
-    kv, qg_packed = lax.optimization_barrier((kv, pack(query, grad_out)))
-    kv_before = lax.ppermute(kv, "z", up)
-    kv_after = lax.ppermute(kv, "z", down)
+    blocks = kv.shape[0]
+    plan = plan_blocks(place, neighbour.T, counts, blocks)
+    kv, qg_packed, plan = lax.optimization_barrier((kv, pack(query, grad_out), plan))
+    kv_first = lax.ppermute(kv, ("z", "core"), out_pairs)
+    kv_second = lax.ppermute(kv, ("z", "core"), in_pairs)
     qg = exchange(qg_packed)
     kv_other = lax.ppermute(kv, "core", swap)
-    kv_before, kv_after, qg = lax.optimization_barrier((kv_before, kv_after, qg))
-    before_other = lax.ppermute(kv_before, "core", swap)
-    after_other = lax.ppermute(kv_after, "core", swap)
-
-    def place():
-        return lax.axis_index("z"), lax.axis_index("core")
-
-    oq, own, other = attend(
-        place,
-        neighbour.T,
-        counts,
-        qg,
-        (kv_before, kv, kv_after, before_other, kv_other, after_other),
+    kv_first, kv_second, qg, kv_other = lax.optimization_barrier(
+        (kv_first, kv_second, qg, kv_other)
     )
+    sides_own = join(kv_first, kv_second)
+    sides_other = lax.ppermute(sides_own, "core", swap)
+    oq, own, other = attend(plan, qg, (kv, sides_own, kv_other, sides_other))
     mine = lax.ppermute(other, "core", swap)
-    to_before, to_after, here = sides(own, mine)
-    from_after = lax.ppermute(to_before, "z", down)
-    from_before = lax.ppermute(to_after, "z", up)
+    to_first, to_second, here = sides(own, mine)
+    from_first = lax.ppermute(to_first, ("z", "core"), in_pairs)
+    from_second = lax.ppermute(to_second, ("z", "core"), out_pairs)
     back_oq = exchange(oq)
-    total = finish(here, from_after, from_before)
+    total = finish(here, from_first, from_second)
     dquery, out = unpack(back_oq)
     dkey, dvalue = unpack(exchange(total))
     return out, dquery, dkey, dvalue

time: 111 us -> 112 us (level); the launches traced: 109 us -> 112 us
  blocking collectives: 0 us -> 14.6 us
  waiting for transfers between devices: 37.6 us -> 30.2 us
  starting transfers between devices: 51.6 us -> 45.3 us
  Pallas kernels: 19 us -> 20.6 us
    all_to_all x0 -> x1, blocking collectives: none -> 14.6 us  [exchange(): lax.all_to_all(packed, HEADS, split_axis=0, concat_axis=0, tiled=True)]
    ppermute x6 -> x5, starting transfers between devices: 27.2 us -> 22.4 us  [the longest x1 9.5 us: on_device(): kv_first = lax.ppermute(kv, ('z', 'core'), out_pairs)]
    all_to_all x4 -> x3, waiting for transfers between devices: 22.1 us -> 18.2 us  [exchange(): lax.all_to_all(packed, HEADS, split_axis=0, concat_axis=0, tiled=True)]
    all_to_all x4 -> x3, starting transfers between devices: 18.3 us -> 14.7 us  [exchange(): lax.all_to_all(packed, HEADS, split_axis=0, concat_axis=0, tiled=True)]
    ppermute x6 -> x5, waiting for transfers between devices: 12.3 us -> 9.05 us  [the longest x1 3.95 us: on_device(): from_second = lax.ppermute(to_second, ('z', 'core'), out_pairs)]
    ppermute x1, starting transfers between devices: 3.96 us -> 5.64 us  [on_device(): kv_other = lax.ppermute(kv, 'core', swap)]
    pallas_call x1 -> x3, Pallas kernels: 10.9 us -> 12.5 us  [the longest x1 9 us: attend(): pl.pallas_call(functools.partial(attend_kernel, variants, size), out_shap...]
  transfers between devices with their start and end apart: 12 -> 10, of which waited for: 7 -> 7; matrix products, arithmetic and copies ran while one was open for 0% -> 0% of each run, Pallas kernels for 4% -> 7%
where the time goes in v3:
time: 112 us
  starting transfers between devices  45.3 us (40%)
  waiting for transfers between devices  30.2 us (27%)
  Pallas kernels  20.6 us (18%)
  blocking collectives  14.6 us (13%)
    all_to_all x3, waiting for transfers between devices, exchange(): lax.all_to_all(packed, HEADS, split_axis=0, concat_axis=0, tiled=True)  18.2 us
    all_to_all x3, starting transfers between devices, exchange(): lax.all_to_all(packed, HEADS, split_axis=0, concat_axis=0, tiled=True)  14.7 us
    all_to_all x1, blocking collectives, exchange(): lax.all_to_all(packed, HEADS, split_axis=0, concat_axis=0, tiled=True)  14.6 us
    ppermute x1, starting transfers between devices, on_device(): kv_first = lax.ppermute(kv, ('z', 'core'), out_pairs)  9.5 us
    pallas_call x1, Pallas kernels, attend(): pl.pallas_call(functools.partial(attend_kernel, variants, size), out_shap...  9 us
    ppermute x1, starting transfers between devices, on_device(): kv_other = lax.ppermute(kv, 'core', swap)  5.64 us
    ppermute x1, starting transfers between devices, on_device(): from_second = lax.ppermute(to_second, ('z', 'core'), out_pairs)  4.57 us
    pallas_call x2, Pallas kernels, pack(): pl.pallas_call(pack_kernel, out_shape=jax.ShapeDtypeStruct(joined, a.dtyp...  4.12 us
  transfers between devices with their start and end apart: 10, of which 7 were waited for; matrix products, arithmetic and copies ran while one was open for 0% of the time, Pallas kernels for 7%

profile of v3, /device:TPU:1, one launch (start us, length us, event | category | flops | bytes accessed | tf_op | source)
XLA Modules:
  0.0 111.5 jit_solution(121203795183790419)
XLA Ops:
  0.6 0.0 copy-start.1
  0.6 0.0 copy-start
  0.7 2.1 %pack.2 = bf16[16,128,128]{2,1,0:T(8,128)(2,1)} custom-call(bf16[128,1024]{1,0:T(8,128)(2,1)} %a_hbm.2, bf16[128,1024]{1,0:T(8,128)(2,1)} %b_hbm.2), custom_call_target="tpu_custom_call" | custom-call | bytes 1048576 | tf_op jit(solution)/shard_map/pack/pallas_call | solution.py:55
  2.7 7.6 %all-to-all-start = ((bf16[16,128,128]{2,1,0:T(8,128)(2,1)}), bf16[16,128,128]{2,1,0:T(8,128)(2,1)S(1)}, u32[]{:S(2)}, u32[]{:S(2)}) async-start(bf16[16,128,128]{2,1,0:T(8,128)(2,1)} %pack.2), calls=%async_computation | async-start | bytes 1048576 | tf_op jit(solution)/shard_map/all_to_all | solution.py:376
  10.3 3.4 %plan.1 = s32[16,16]{1,0:T(8,128)S(1)} custom-call(s32[8,512]{1,0:T(8,128)S(1)} %bitcast.1, s32[512]{0:T(512)S(1)} %copy-done.1), custom_call_target="tpu_custom_call" | custom-call | bytes 1048576 | tf_op jit(solution)/shard_map/plan/pallas_call | solution.py:191
  13.7 2.0 %pack.3 = bf16[16,128,128]{2,1,0:T(8,128)(2,1)} custom-call(bf16[128,1024]{1,0:T(8,128)(2,1)} %a_hbm.3, bf16[128,1024]{1,0:T(8,128)(2,1)} %b_hbm.3), custom_call_target="tpu_custom_call" | custom-call | bytes 1048576 | tf_op jit(solution)/shard_map/pack/pallas_call | solution.py:55
  15.8 3.7 %all-to-all-done.rest_0_ = bf16[16,128,128]{2,1,0:T(8,128)(2,1)S(1)} async-done(((bf16[16,128,128]{2,1,0:T(8,128)(2,1)}), bf16[16,128,128]{2,1,0:T(8,128)(2,1)S(1)}, u32[]{:S(2)}, u32[]{:S(2)}) %all-to-all-start) | async-done | bytes 524320 | tf_op jit(solution)/shard_map/all_to_all | solution.py:376
  19.5 5.6 %collective-permute-start.2 = (bf16[16,128,128]{2,1,0:T(8,128)(2,1)S(1)}, bf16[16,128,128]{2,1,0:T(8,128)(2,1)S(1)}, u32[]{:S(2)}, u32[]{:S(2)}) collective-permute-start(bf16[16,128,128]{2,1,0:T(8,128)(2,1)S(1)} %all-to-all-done.rest_0_), channel_id=1, source_target_pairs={{0,1},{1,0},{2,3},{3,2},{4,5},{5,4},{6,7},{7,6},{8,9},{9,8},{10,11... | collective-permute-start | bytes 1572872 | tf_op jit(solution)/shard_map/ppermute | solution.py:385
  25.2 3.1 %collective-permute-start.1 = (bf16[16,128,128]{2,1,0:T(8,128)(2,1)S(1)}, bf16[16,128,128]{2,1,0:T(8,128)(2,1)S(1)}, u32[]{:S(2)}, u32[]{:S(2)}) collective-permute-start(bf16[16,128,128]{2,1,0:T(8,128)(2,1)S(1)} %all-to-all-done.rest_0_), channel_id=1, source_target_pairs={{32,0},{481,1},{64,32},{1,33},{96,64},{33,65},{128,96},{65,97},{16... | collective-permute-start | bytes 1572872 | tf_op jit(solution)/shard_map/ppermute | solution.py:383
  28.3 9.5 %collective-permute-start = (bf16[16,128,128]{2,1,0:T(8,128)(2,1)S(1)}, bf16[16,128,128]{2,1,0:T(8,128)(2,1)S(1)}, u32[]{:S(2)}, u32[]{:S(2)}) collective-permute-start(bf16[16,128,128]{2,1,0:T(8,128)(2,1)S(1)} %all-to-all-done.rest_0_), channel_id=1, source_target_pairs={{0,32},{1,481},{32,64},{33,1},{64,96},{65,33},{96,128},{97,65},{12... | collective-permute-start | bytes 1572872 | tf_op jit(solution)/shard_map/ppermute | solution.py:382
  37.8 14.6 %all_to_all.20.qg_ref = bf16[16,128,128]{2,1,0:T(8,128)(2,1)S(1)} all-to-all(bf16[16,128,128]{2,1,0:T(8,128)(2,1)} %pack.3), channel_id=1, replica_groups=mesh['z'=16,'yl'=2,'yh'=2,'x'=4,'core'=2] {'yl','yh','x'}, dimensions={0} | all-to-all | bytes 1048576 | tf_op jit(solution)/shard_map/all_to_all | solution.py:376
  52.4 0.0 collective-permute-done.2.rest_2_
  52.4 0.0 collective-permute-done.1.b_ref
  52.4 0.0 collective-permute-done.a_ref
  52.4 0.1 join.1.rest_1_
  52.4 3.4 %collective-permute-start.3 = (bf16[32,128,128]{2,1,0:T(8,128)(2,1)S(1)}, bf16[32,128,128]{2,1,0:T(8,128)(2,1)S(1)}, u32[]{:S(2)}, u32[]{:S(2)}) collective-permute-start(bf16[32,128,128]{2,1,0:T(8,128)(2,1)S(1)} %join.1.rest_1_), channel_id=1, source_target_pairs={{0,1},{1,0},{2,3},{3,2},{4,5},{5,4},{6,7},{7,6},{8,9},{9,8},{10,11... | collective-permute-start | bytes 3145736 | tf_op jit(solution)/shard_map/ppermute | solution.py:390
  55.8 2.3 %collective-permute-done.3.rest_3_ = bf16[32,128,128]{2,1,0:T(8,128)(2,1)S(1)} collective-permute-done((bf16[32,128,128]{2,1,0:T(8,128)(2,1)S(1)}, bf16[32,128,128]{2,1,0:T(8,128)(2,1)S(1)}, u32[]{:S(2)}, u32[]{:S(2)}) %collective-permute-start.3) | collective-permute-done | bytes 1048608 | tf_op jit(solution)/shard_map/ppermute | solution.py:390
  58.1 9.0 %attend.1 = (bf16[16,128,128]{2,1,0:T(8,128)(2,1)}, f32[48,128,128]{2,1,0:T(8,128)S(1)}, bf16[48,128,128]{2,1,0:T(8,128)(2,1)S(1)}) custom-call(s32[16,16]{1,0:T(8,128)S(1)} %plan.1, bf16[16,128,128]{2,1,0:T(8,128)(2,1)S(1)} %all_to_all.20.qg_ref, bf16[16,128,128]{2,1,0:T(8,128)(2,1)S(1)} %all-to-all-done.rest_0_, bf16[32,128,128]{2,1,0:T(8,128)(2,1)S(1)} %join.1.rest_1_, ...), custom_call_target="tpu_custom_call" | custom-call | flops 838860800 | bytes 8388608 | tf_op jit(solution)/shard_map/attend/pallas_call | solution.py:334
  67.1 2.5 %collective-permute-start.4 = (bf16[48,128,128]{2,1,0:T(8,128)(2,1)S(1)}, bf16[48,128,128]{2,1,0:T(8,128)(2,1)S(1)}, u32[]{:S(2)}, u32[]{:S(2)}) collective-permute-start(bf16[48,128,128]{2,1,0:T(8,128)(2,1)S(1)} %get-tuple-element.32), channel_id=1, source_target_pairs={{0,1},{1,0},{2,3},{3,2},{4,5},{5,4},{6,7},{7,6},{8,9},{9,8},{10,11... | collective-permute-start | bytes 4718600 | tf_op jit(solution)/shard_map/ppermute | solution.py:392
  69.6 3.0 %collective-permute-done.4.mine_ref = bf16[48,128,128]{2,1,0:T(8,128)(2,1)S(1)} collective-permute-done((bf16[48,128,128]{2,1,0:T(8,128)(2,1)S(1)}, bf16[48,128,128]{2,1,0:T(8,128)(2,1)S(1)}, u32[]{:S(2)}, u32[]{:S(2)}) %collective-permute-start.4) | collective-permute-done | bytes 1572896 | tf_op jit(solution)/shard_map/ppermute | solution.py:392
  72.6 1.1 sides.1
  73.7 1.9 %collective-permute-start.5 = (bf16[16,128,128]{2,1,0:T(8,128)(2,1)}, bf16[16,128,128]{2,1,0:T(8,128)(2,1)S(1)}, u32[]{:S(2)}, u32[]{:S(2)}) collective-permute-start(bf16[16,128,128]{2,1,0:T(8,128)(2,1)} %get-tuple-element.34), channel_id=1, source_target_pairs={{32,0},{481,1},{64,32},{1,33},{96,64},{33,65},{128,96},{65,97},{16... | collective-permute-start | bytes 1572872 | tf_op jit(solution)/shard_map/ppermute | solution.py:394
  75.7 4.6 %collective-permute-start.6 = (bf16[16,128,128]{2,1,0:T(8,128)(2,1)S(1)}, bf16[16,128,128]{2,1,0:T(8,128)(2,1)S(1)}, u32[]{:S(2)}, u32[]{:S(2)}) collective-permute-start(bf16[16,128,128]{2,1,0:T(8,128)(2,1)S(1)} %get-tuple-element.35), channel_id=1, source_target_pairs={{0,32},{1,481},{32,64},{33,1},{64,96},{65,33},{96,128},{97,65},{12... | collective-permute-start | bytes 1572872 | tf_op jit(solution)/shard_map/ppermute | solution.py:395
  80.2 3.6 %all-to-all-start.2 = ((bf16[16,128,128]{2,1,0:T(8,128)(2,1)}), bf16[16,128,128]{2,1,0:T(8,128)(2,1)S(1)}, u32[]{:S(2)}, u32[]{:S(2)}) async-start(bf16[16,128,128]{2,1,0:T(8,128)(2,1)} %get-tuple-element.28), calls=%async_computation.2 | async-start | bytes 1048576 | tf_op jit(solution)/shard_map/all_to_all | solution.py:376
  83.8 2.8 %collective-permute-done.5.first_ref = bf16[16,128,128]{2,1,0:T(8,128)(2,1)S(1)} collective-permute-done((bf16[16,128,128]{2,1,0:T(8,128)(2,1)}, bf16[16,128,128]{2,1,0:T(8,128)(2,1)S(1)}, u32[]{:S(2)}, u32[]{:S(2)}) %collective-permute-start.5) | collective-permute-done | bytes 524320 | tf_op jit(solution)/shard_map/ppermute | solution.py:394
  86.7 4.0 %collective-permute-done.6.second_ref = bf16[16,128,128]{2,1,0:T(8,128)(2,1)S(1)} collective-permute-done((bf16[16,128,128]{2,1,0:T(8,128)(2,1)S(1)}, bf16[16,128,128]{2,1,0:T(8,128)(2,1)S(1)}, u32[]{:S(2)}, u32[]{:S(2)}) %collective-permute-start.6) | collective-permute-done | bytes 524320 | tf_op jit(solution)/shard_map/ppermute | solution.py:395
  90.6 0.9 finish.1
  91.5 4.4 %all-to-all-done.2.i_ref = bf16[16,128,128]{2,1,0:T(8,128)(2,1)S(1)} async-done(((bf16[16,128,128]{2,1,0:T(8,128)(2,1)}), bf16[16,128,128]{2,1,0:T(8,128)(2,1)S(1)}, u32[]{:S(2)}, u32[]{:S(2)}) %all-to-all-start.2) | async-done | bytes 524320 | tf_op jit(solution)/shard_map/all_to_all | solution.py:376
  95.9 3.6 %all-to-all-start.3 = ((bf16[16,128,128]{2,1,0:T(8,128)(2,1)}), bf16[16,128,128]{2,1,0:T(8,128)(2,1)S(1)}, u32[]{:S(2)}, u32[]{:S(2)}) async-start(bf16[16,128,128]{2,1,0:T(8,128)(2,1)} %finish.1), calls=%async_computation.3 | async-start | bytes 1048576 | tf_op jit(solution)/shard_map/all_to_all | solution.py:376
  99.5 1.0 unpack.2
  100.5 10.1 %all-to-all-done.3.i_ref = bf16[16,128,128]{2,1,0:T(8,128)(2,1)S(1)} async-done(((bf16[16,128,128]{2,1,0:T(8,128)(2,1)}), bf16[16,128,128]{2,1,0:T(8,128)(2,1)S(1)}, u32[]{:S(2)}, u32[]{:S(2)}) %all-to-all-start.3) | async-done | bytes 524320 | tf_op jit(solution)/shard_map/all_to_all | solution.py:376
  110.5 1.0 unpack.3
  (2 shorter events, 0.0 us)
Async XLA Ops:
  0.6 9.7 %copy-start.1 = (s32[512]{0:T(512)S(1)}, s32[512]{0:T(512)}, u32[]{:S(2)}) copy-start(s32[512]{0:T(512)} %cnt.1) | copy-start | bytes 6148
  0.6 9.7 %copy-start = (s32[512,8]{0,1:T(8,128)S(1)}, s32[512,8]{0,1:T(8,128)}, u32[]{:S(2)}) copy-start(s32[512,8]{0,1:T(8,128)} %param.10) | copy-start | bytes 49156
  2.7 16.8 %all-to-all-start = ((bf16[16,128,128]{2,1,0:T(8,128)(2,1)}), bf16[16,128,128]{2,1,0:T(8,128)(2,1)S(1)}, u32[]{:S(2)}, u32[]{:S(2)}) async-start(bf16[16,128,128]{2,1,0:T(8,128)(2,1)} %pack.2), calls=%async_computation | async-start | bytes 1048576 | tf_op jit(solution)/shard_map/all_to_all | solution.py:376
  19.5 32.8 %collective-permute-start.2 = (bf16[16,128,128]{2,1,0:T(8,128)(2,1)S(1)}, bf16[16,128,128]{2,1,0:T(8,128)(2,1)S(1)}, u32[]{:S(2)}, u32[]{:S(2)}) collective-permute-start(bf16[16,128,128]{2,1,0:T(8,128)(2,1)S(1)} %all-to-all-done.rest_0_), channel_id=1, source_target_pairs={{0,1},{1,0},{2,3},{3,2},{4,5},{5,4},{6,7},{7,6},{8,9},{9,8},{10,11... | collective-permute-start | bytes 1572872 | tf_op jit(solution)/shard_map/ppermute | solution.py:385
  25.2 27.2 %collective-permute-start.1 = (bf16[16,128,128]{2,1,0:T(8,128)(2,1)S(1)}, bf16[16,128,128]{2,1,0:T(8,128)(2,1)S(1)}, u32[]{:S(2)}, u32[]{:S(2)}) collective-permute-start(bf16[16,128,128]{2,1,0:T(8,128)(2,1)S(1)} %all-to-all-done.rest_0_), channel_id=1, source_target_pairs={{32,0},{481,1},{64,32},{1,33},{96,64},{33,65},{128,96},{65,97},{16... | collective-permute-start | bytes 1572872 | tf_op jit(solution)/shard_map/ppermute | solution.py:383
  28.3 24.1 %collective-permute-start = (bf16[16,128,128]{2,1,0:T(8,128)(2,1)S(1)}, bf16[16,128,128]{2,1,0:T(8,128)(2,1)S(1)}, u32[]{:S(2)}, u32[]{:S(2)}) collective-permute-start(bf16[16,128,128]{2,1,0:T(8,128)(2,1)S(1)} %all-to-all-done.rest_0_), channel_id=1, source_target_pairs={{0,32},{1,481},{32,64},{33,1},{64,96},{65,33},{96,128},{97,65},{12... | collective-permute-start | bytes 1572872 | tf_op jit(solution)/shard_map/ppermute | solution.py:382
  52.4 5.6 %collective-permute-start.3 = (bf16[32,128,128]{2,1,0:T(8,128)(2,1)S(1)}, bf16[32,128,128]{2,1,0:T(8,128)(2,1)S(1)}, u32[]{:S(2)}, u32[]{:S(2)}) collective-permute-start(bf16[32,128,128]{2,1,0:T(8,128)(2,1)S(1)} %join.1.rest_1_), channel_id=1, source_target_pairs={{0,1},{1,0},{2,3},{3,2},{4,5},{5,4},{6,7},{7,6},{8,9},{9,8},{10,11... | collective-permute-start | bytes 3145736 | tf_op jit(solution)/shard_map/ppermute | solution.py:390
  67.1 5.6 %collective-permute-start.4 = (bf16[48,128,128]{2,1,0:T(8,128)(2,1)S(1)}, bf16[48,128,128]{2,1,0:T(8,128)(2,1)S(1)}, u32[]{:S(2)}, u32[]{:S(2)}) collective-permute-start(bf16[48,128,128]{2,1,0:T(8,128)(2,1)S(1)} %get-tuple-element.32), channel_id=1, source_target_pairs={{0,1},{1,0},{2,3},{3,2},{4,5},{5,4},{6,7},{7,6},{8,9},{9,8},{10,11... | collective-permute-start | bytes 4718600 | tf_op jit(solution)/shard_map/ppermute | solution.py:392
  73.7 12.9 %collective-permute-start.5 = (bf16[16,128,128]{2,1,0:T(8,128)(2,1)}, bf16[16,128,128]{2,1,0:T(8,128)(2,1)S(1)}, u32[]{:S(2)}, u32[]{:S(2)}) collective-permute-start(bf16[16,128,128]{2,1,0:T(8,128)(2,1)} %get-tuple-element.34), channel_id=1, source_target_pairs={{32,0},{481,1},{64,32},{1,33},{96,64},{33,65},{128,96},{65,97},{16... | collective-permute-start | bytes 1572872 | tf_op jit(solution)/shard_map/ppermute | solution.py:394
  75.7 15.0 %collective-permute-start.6 = (bf16[16,128,128]{2,1,0:T(8,128)(2,1)S(1)}, bf16[16,128,128]{2,1,0:T(8,128)(2,1)S(1)}, u32[]{:S(2)}, u32[]{:S(2)}) collective-permute-start(bf16[16,128,128]{2,1,0:T(8,128)(2,1)S(1)} %get-tuple-element.35), channel_id=1, source_target_pairs={{0,32},{1,481},{32,64},{33,1},{64,96},{65,33},{96,128},{97,65},{12... | collective-permute-start | bytes 1572872 | tf_op jit(solution)/shard_map/ppermute | solution.py:395
  80.2 15.7 %all-to-all-start.2 = ((bf16[16,128,128]{2,1,0:T(8,128)(2,1)}), bf16[16,128,128]{2,1,0:T(8,128)(2,1)S(1)}, u32[]{:S(2)}, u32[]{:S(2)}) async-start(bf16[16,128,128]{2,1,0:T(8,128)(2,1)} %get-tuple-element.28), calls=%async_computation.2 | async-start | bytes 1048576 | tf_op jit(solution)/shard_map/all_to_all | solution.py:376
  95.9 14.6 %all-to-all-start.3 = ((bf16[16,128,128]{2,1,0:T(8,128)(2,1)}), bf16[16,128,128]{2,1,0:T(8,128)(2,1)S(1)}, u32[]{:S(2)}, u32[]{:S(2)}) async-start(bf16[16,128,128]{2,1,0:T(8,128)(2,1)} %finish.1), calls=%async_computation.3 | async-start | bytes 1048576 | tf_op jit(solution)/shard_map/all_to_all | solution.py:376

commit v4 on v3

--- a/solution.py
+++ b/solution.py
@@ -154,6 +154,8 @@
     plane_blocks = 2 * blocks
     all_blocks = cnt.shape[0]
     first = (z - 1) * plane_blocks
+    shift = plane_blocks.bit_length() - 1
+    assert plane_blocks == 1 << shift and all_blocks & (all_blocks - 1) == 0
 
     def block_of(s):
         return z * plane_blocks + 2 * s + core
@@ -178,13 +180,12 @@
         plan[at, NNB] = s
         plan[at, NNB + 1] = c
         for j in range(NNB):
-            rel = lax.rem(nbr[j, b] - first + all_blocks, all_blocks)
-            side = lax.rem(rel + core, 2)
-            plane = lax.div(rel, plane_blocks)
-            slot = jnp.where(lax.rem(rel, 2) == 1, PLANES - 1 - plane, plane)
-            plan[at, j] = (side * PLANES + slot) * blocks + lax.div(
-                lax.rem(rel, plane_blocks), 2
-            )
+            rel = (nbr[j, b] - first) & (all_blocks - 1)
+            plane = rel >> shift
+            slot = plane + (rel & 1) * (PLANES - 1 - 2 * plane)
+            side = (rel + core) & 1
+            within = (rel & (plane_blocks - 1)) >> 1
+            plan[at, j] = (side * PLANES + slot) * blocks + within
 
 
 def plan_blocks(place, nbr_t, counts, blocks):

time: 112 us -> 112 us (level)
  transfers between devices with their start and end apart: 10 -> 10, of which waited for: 7 -> 7; matrix products, arithmetic and copies ran while one was open for 0% -> 0% of each run, Pallas kernels for 7% -> 6%
where the time goes in v4:
time: 112 us
  starting transfers between devices  45.3 us (40%)
  waiting for transfers between devices  31 us (28%)
  Pallas kernels  19.8 us (18%)
  blocking collectives  14.6 us (13%)
    all_to_all x3, waiting for transfers between devices, exchange(): lax.all_to_all(packed, HEADS, split_axis=0, concat_axis=0, tiled=True)  18.9 us
    all_to_all x3, starting transfers between devices, exchange(): lax.all_to_all(packed, HEADS, split_axis=0, concat_axis=0, tiled=True)  14.7 us
    all_to_all x1, blocking collectives, exchange(): lax.all_to_all(packed, HEADS, split_axis=0, concat_axis=0, tiled=True)  14.6 us
    ppermute x1, starting transfers between devices, on_device(): kv_first = lax.ppermute(kv, ('z', 'core'), out_pairs)  9.5 us
    pallas_call x1, Pallas kernels, attend(): pl.pallas_call(functools.partial(attend_kernel, variants, size), out_shap...  9 us
    ppermute x1, starting transfers between devices, on_device(): kv_other = lax.ppermute(kv, 'core', swap)  5.64 us
    ppermute x1, starting transfers between devices, on_device(): from_second = lax.ppermute(to_second, ('z', 'core'), out_pairs)  4.57 us
    pallas_call x2, Pallas kernels, pack(): pl.pallas_call(pack_kernel, out_shape=jax.ShapeDtypeStruct(joined, a.dtyp...  4.12 us
  transfers between devices with their start and end apart: 10, of which 7 were waited for; matrix products, arithmetic and copies ran while one was open for 0% of the time, Pallas kernels for 6%

profile of v4, /device:TPU:1, one launch (start us, length us, event | category | flops | bytes accessed | tf_op | source)
XLA Modules:
  0.0 111.5 jit_solution(15327752529901865186)
XLA Ops:
  0.6 0.0 copy-start.1
  0.6 0.0 copy-start
  0.7 2.1 %pack.2 = bf16[16,128,128]{2,1,0:T(8,128)(2,1)} custom-call(bf16[128,1024]{1,0:T(8,128)(2,1)} %a_hbm.2, bf16[128,1024]{1,0:T(8,128)(2,1)} %b_hbm.2), custom_call_target="tpu_custom_call" | custom-call | bytes 1048576 | tf_op jit(solution)/shard_map/pack/pallas_call | solution.py:55
  2.7 7.6 %all-to-all-start = ((bf16[16,128,128]{2,1,0:T(8,128)(2,1)}), bf16[16,128,128]{2,1,0:T(8,128)(2,1)S(1)}, u32[]{:S(2)}, u32[]{:S(2)}) async-start(bf16[16,128,128]{2,1,0:T(8,128)(2,1)} %pack.2), calls=%async_computation | async-start | bytes 1048576 | tf_op jit(solution)/shard_map/all_to_all | solution.py:377
  10.3 2.6 %plan.1 = s32[16,16]{1,0:T(8,128)S(1)} custom-call(s32[8,512]{1,0:T(8,128)S(1)} %bitcast.1, s32[512]{0:T(512)S(1)} %copy-done.1), custom_call_target="tpu_custom_call" | custom-call | bytes 1048576 | tf_op jit(solution)/shard_map/plan/pallas_call | solution.py:192
  13.0 2.0 %pack.3 = bf16[16,128,128]{2,1,0:T(8,128)(2,1)} custom-call(bf16[128,1024]{1,0:T(8,128)(2,1)} %a_hbm.3, bf16[128,1024]{1,0:T(8,128)(2,1)} %b_hbm.3), custom_call_target="tpu_custom_call" | custom-call | bytes 1048576 | tf_op jit(solution)/shard_map/pack/pallas_call | solution.py:55
  15.0 4.5 %all-to-all-done.rest_0_ = bf16[16,128,128]{2,1,0:T(8,128)(2,1)S(1)} async-done(((bf16[16,128,128]{2,1,0:T(8,128)(2,1)}), bf16[16,128,128]{2,1,0:T(8,128)(2,1)S(1)}, u32[]{:S(2)}, u32[]{:S(2)}) %all-to-all-start) | async-done | bytes 524320 | tf_op jit(solution)/shard_map/all_to_all | solution.py:377
  19.5 5.6 %collective-permute-start.2 = (bf16[16,128,128]{2,1,0:T(8,128)(2,1)S(1)}, bf16[16,128,128]{2,1,0:T(8,128)(2,1)S(1)}, u32[]{:S(2)}, u32[]{:S(2)}) collective-permute-start(bf16[16,128,128]{2,1,0:T(8,128)(2,1)S(1)} %all-to-all-done.rest_0_), channel_id=1, source_target_pairs={{0,1},{1,0},{2,3},{3,2},{4,5},{5,4},{6,7},{7,6},{8,9},{9,8},{10,11... | collective-permute-start | bytes 1572872 | tf_op jit(solution)/shard_map/ppermute | solution.py:386
  25.2 3.1 %collective-permute-start.1 = (bf16[16,128,128]{2,1,0:T(8,128)(2,1)S(1)}, bf16[16,128,128]{2,1,0:T(8,128)(2,1)S(1)}, u32[]{:S(2)}, u32[]{:S(2)}) collective-permute-start(bf16[16,128,128]{2,1,0:T(8,128)(2,1)S(1)} %all-to-all-done.rest_0_), channel_id=1, source_target_pairs={{32,0},{481,1},{64,32},{1,33},{96,64},{33,65},{128,96},{65,97},{16... | collective-permute-start | bytes 1572872 | tf_op jit(solution)/shard_map/ppermute | solution.py:384
  28.3 9.5 %collective-permute-start = (bf16[16,128,128]{2,1,0:T(8,128)(2,1)S(1)}, bf16[16,128,128]{2,1,0:T(8,128)(2,1)S(1)}, u32[]{:S(2)}, u32[]{:S(2)}) collective-permute-start(bf16[16,128,128]{2,1,0:T(8,128)(2,1)S(1)} %all-to-all-done.rest_0_), channel_id=1, source_target_pairs={{0,32},{1,481},{32,64},{33,1},{64,96},{65,33},{96,128},{97,65},{12... | collective-permute-start | bytes 1572872 | tf_op jit(solution)/shard_map/ppermute | solution.py:383
  37.8 14.6 %all_to_all.20.qg_ref = bf16[16,128,128]{2,1,0:T(8,128)(2,1)S(1)} all-to-all(bf16[16,128,128]{2,1,0:T(8,128)(2,1)} %pack.3), channel_id=1, replica_groups=mesh['z'=16,'yl'=2,'yh'=2,'x'=4,'core'=2] {'yl','yh','x'}, dimensions={0} | all-to-all | bytes 1048576 | tf_op jit(solution)/shard_map/all_to_all | solution.py:377
  52.4 0.0 collective-permute-done.2.rest_2_
  52.4 0.0 collective-permute-done.1.b_ref
  52.4 0.0 collective-permute-done.a_ref
  52.4 0.1 join.1.rest_1_
  52.4 3.4 %collective-permute-start.3 = (bf16[32,128,128]{2,1,0:T(8,128)(2,1)S(1)}, bf16[32,128,128]{2,1,0:T(8,128)(2,1)S(1)}, u32[]{:S(2)}, u32[]{:S(2)}) collective-permute-start(bf16[32,128,128]{2,1,0:T(8,128)(2,1)S(1)} %join.1.rest_1_), channel_id=1, source_target_pairs={{0,1},{1,0},{2,3},{3,2},{4,5},{5,4},{6,7},{7,6},{8,9},{9,8},{10,11... | collective-permute-start | bytes 3145736 | tf_op jit(solution)/shard_map/ppermute | solution.py:391
  55.8 2.3 %collective-permute-done.3.rest_3_ = bf16[32,128,128]{2,1,0:T(8,128)(2,1)S(1)} collective-permute-done((bf16[32,128,128]{2,1,0:T(8,128)(2,1)S(1)}, bf16[32,128,128]{2,1,0:T(8,128)(2,1)S(1)}, u32[]{:S(2)}, u32[]{:S(2)}) %collective-permute-start.3) | collective-permute-done | bytes 1048608 | tf_op jit(solution)/shard_map/ppermute | solution.py:391
  58.1 9.0 %attend.1 = (bf16[16,128,128]{2,1,0:T(8,128)(2,1)}, f32[48,128,128]{2,1,0:T(8,128)S(1)}, bf16[48,128,128]{2,1,0:T(8,128)(2,1)S(1)}) custom-call(s32[16,16]{1,0:T(8,128)S(1)} %plan.1, bf16[16,128,128]{2,1,0:T(8,128)(2,1)S(1)} %all_to_all.20.qg_ref, bf16[16,128,128]{2,1,0:T(8,128)(2,1)S(1)} %all-to-all-done.rest_0_, bf16[32,128,128]{2,1,0:T(8,128)(2,1)S(1)} %join.1.rest_1_, ...), custom_call_target="tpu_custom_call" | custom-call | flops 838860800 | bytes 8388608 | tf_op jit(solution)/shard_map/attend/pallas_call | solution.py:335
  67.1 2.5 %collective-permute-start.4 = (bf16[48,128,128]{2,1,0:T(8,128)(2,1)S(1)}, bf16[48,128,128]{2,1,0:T(8,128)(2,1)S(1)}, u32[]{:S(2)}, u32[]{:S(2)}) collective-permute-start(bf16[48,128,128]{2,1,0:T(8,128)(2,1)S(1)} %get-tuple-element.32), channel_id=1, source_target_pairs={{0,1},{1,0},{2,3},{3,2},{4,5},{5,4},{6,7},{7,6},{8,9},{9,8},{10,11... | collective-permute-start | bytes 4718600 | tf_op jit(solution)/shard_map/ppermute | solution.py:393
  69.6 3.0 %collective-permute-done.4.mine_ref = bf16[48,128,128]{2,1,0:T(8,128)(2,1)S(1)} collective-permute-done((bf16[48,128,128]{2,1,0:T(8,128)(2,1)S(1)}, bf16[48,128,128]{2,1,0:T(8,128)(2,1)S(1)}, u32[]{:S(2)}, u32[]{:S(2)}) %collective-permute-start.4) | collective-permute-done | bytes 1572896 | tf_op jit(solution)/shard_map/ppermute | solution.py:393
  72.6 1.1 sides.1
  73.7 1.9 %collective-permute-start.5 = (bf16[16,128,128]{2,1,0:T(8,128)(2,1)}, bf16[16,128,128]{2,1,0:T(8,128)(2,1)S(1)}, u32[]{:S(2)}, u32[]{:S(2)}) collective-permute-start(bf16[16,128,128]{2,1,0:T(8,128)(2,1)} %get-tuple-element.34), channel_id=1, source_target_pairs={{32,0},{481,1},{64,32},{1,33},{96,64},{33,65},{128,96},{65,97},{16... | collective-permute-start | bytes 1572872 | tf_op jit(solution)/shard_map/ppermute | solution.py:395
  75.7 4.6 %collective-permute-start.6 = (bf16[16,128,128]{2,1,0:T(8,128)(2,1)S(1)}, bf16[16,128,128]{2,1,0:T(8,128)(2,1)S(1)}, u32[]{:S(2)}, u32[]{:S(2)}) collective-permute-start(bf16[16,128,128]{2,1,0:T(8,128)(2,1)S(1)} %get-tuple-element.35), channel_id=1, source_target_pairs={{0,32},{1,481},{32,64},{33,1},{64,96},{65,33},{96,128},{97,65},{12... | collective-permute-start | bytes 1572872 | tf_op jit(solution)/shard_map/ppermute | solution.py:396
  80.2 3.6 %all-to-all-start.2 = ((bf16[16,128,128]{2,1,0:T(8,128)(2,1)}), bf16[16,128,128]{2,1,0:T(8,128)(2,1)S(1)}, u32[]{:S(2)}, u32[]{:S(2)}) async-start(bf16[16,128,128]{2,1,0:T(8,128)(2,1)} %get-tuple-element.28), calls=%async_computation.2 | async-start | bytes 1048576 | tf_op jit(solution)/shard_map/all_to_all | solution.py:377
  83.8 2.8 %collective-permute-done.5.first_ref = bf16[16,128,128]{2,1,0:T(8,128)(2,1)S(1)} collective-permute-done((bf16[16,128,128]{2,1,0:T(8,128)(2,1)}, bf16[16,128,128]{2,1,0:T(8,128)(2,1)S(1)}, u32[]{:S(2)}, u32[]{:S(2)}) %collective-permute-start.5) | collective-permute-done | bytes 524320 | tf_op jit(solution)/shard_map/ppermute | solution.py:395
  86.7 4.0 %collective-permute-done.6.second_ref = bf16[16,128,128]{2,1,0:T(8,128)(2,1)S(1)} collective-permute-done((bf16[16,128,128]{2,1,0:T(8,128)(2,1)S(1)}, bf16[16,128,128]{2,1,0:T(8,128)(2,1)S(1)}, u32[]{:S(2)}, u32[]{:S(2)}) %collective-permute-start.6) | collective-permute-done | bytes 524320 | tf_op jit(solution)/shard_map/ppermute | solution.py:396
  90.6 0.9 finish.1
  91.5 4.4 %all-to-all-done.2.i_ref = bf16[16,128,128]{2,1,0:T(8,128)(2,1)S(1)} async-done(((bf16[16,128,128]{2,1,0:T(8,128)(2,1)}), bf16[16,128,128]{2,1,0:T(8,128)(2,1)S(1)}, u32[]{:S(2)}, u32[]{:S(2)}) %all-to-all-start.2) | async-done | bytes 524320 | tf_op jit(solution)/shard_map/all_to_all | solution.py:377
  95.9 3.6 %all-to-all-start.3 = ((bf16[16,128,128]{2,1,0:T(8,128)(2,1)}), bf16[16,128,128]{2,1,0:T(8,128)(2,1)S(1)}, u32[]{:S(2)}, u32[]{:S(2)}) async-start(bf16[16,128,128]{2,1,0:T(8,128)(2,1)} %finish.1), calls=%async_computation.3 | async-start | bytes 1048576 | tf_op jit(solution)/shard_map/all_to_all | solution.py:377
  99.5 1.0 unpack.2
  100.5 10.1 %all-to-all-done.3.i_ref = bf16[16,128,128]{2,1,0:T(8,128)(2,1)S(1)} async-done(((bf16[16,128,128]{2,1,0:T(8,128)(2,1)}), bf16[16,128,128]{2,1,0:T(8,128)(2,1)S(1)}, u32[]{:S(2)}, u32[]{:S(2)}) %all-to-all-start.3) | async-done | bytes 524320 | tf_op jit(solution)/shard_map/all_to_all | solution.py:377
  110.5 1.0 unpack.3
  (2 shorter events, 0.0 us)
Async XLA Ops:
  0.6 9.7 %copy-start.1 = (s32[512]{0:T(512)S(1)}, s32[512]{0:T(512)}, u32[]{:S(2)}) copy-start(s32[512]{0:T(512)} %cnt.1) | copy-start | bytes 6148
  0.6 9.7 %copy-start = (s32[512,8]{0,1:T(8,128)S(1)}, s32[512,8]{0,1:T(8,128)}, u32[]{:S(2)}) copy-start(s32[512,8]{0,1:T(8,128)} %param.10) | copy-start | bytes 49156
  2.7 16.8 %all-to-all-start = ((bf16[16,128,128]{2,1,0:T(8,128)(2,1)}), bf16[16,128,128]{2,1,0:T(8,128)(2,1)S(1)}, u32[]{:S(2)}, u32[]{:S(2)}) async-start(bf16[16,128,128]{2,1,0:T(8,128)(2,1)} %pack.2), calls=%async_computation | async-start | bytes 1048576 | tf_op jit(solution)/shard_map/all_to_all | solution.py:377
  19.5 32.8 %collective-permute-start.2 = (bf16[16,128,128]{2,1,0:T(8,128)(2,1)S(1)}, bf16[16,128,128]{2,1,0:T(8,128)(2,1)S(1)}, u32[]{:S(2)}, u32[]{:S(2)}) collective-permute-start(bf16[16,128,128]{2,1,0:T(8,128)(2,1)S(1)} %all-to-all-done.rest_0_), channel_id=1, source_target_pairs={{0,1},{1,0},{2,3},{3,2},{4,5},{5,4},{6,7},{7,6},{8,9},{9,8},{10,11... | collective-permute-start | bytes 1572872 | tf_op jit(solution)/shard_map/ppermute | solution.py:386
  25.2 27.2 %collective-permute-start.1 = (bf16[16,128,128]{2,1,0:T(8,128)(2,1)S(1)}, bf16[16,128,128]{2,1,0:T(8,128)(2,1)S(1)}, u32[]{:S(2)}, u32[]{:S(2)}) collective-permute-start(bf16[16,128,128]{2,1,0:T(8,128)(2,1)S(1)} %all-to-all-done.rest_0_), channel_id=1, source_target_pairs={{32,0},{481,1},{64,32},{1,33},{96,64},{33,65},{128,96},{65,97},{16... | collective-permute-start | bytes 1572872 | tf_op jit(solution)/shard_map/ppermute | solution.py:384
  28.3 24.1 %collective-permute-start = (bf16[16,128,128]{2,1,0:T(8,128)(2,1)S(1)}, bf16[16,128,128]{2,1,0:T(8,128)(2,1)S(1)}, u32[]{:S(2)}, u32[]{:S(2)}) collective-permute-start(bf16[16,128,128]{2,1,0:T(8,128)(2,1)S(1)} %all-to-all-done.rest_0_), channel_id=1, source_target_pairs={{0,32},{1,481},{32,64},{33,1},{64,96},{65,33},{96,128},{97,65},{12... | collective-permute-start | bytes 1572872 | tf_op jit(solution)/shard_map/ppermute | solution.py:383
  52.4 5.6 %collective-permute-start.3 = (bf16[32,128,128]{2,1,0:T(8,128)(2,1)S(1)}, bf16[32,128,128]{2,1,0:T(8,128)(2,1)S(1)}, u32[]{:S(2)}, u32[]{:S(2)}) collective-permute-start(bf16[32,128,128]{2,1,0:T(8,128)(2,1)S(1)} %join.1.rest_1_), channel_id=1, source_target_pairs={{0,1},{1,0},{2,3},{3,2},{4,5},{5,4},{6,7},{7,6},{8,9},{9,8},{10,11... | collective-permute-start | bytes 3145736 | tf_op jit(solution)/shard_map/ppermute | solution.py:391
  67.1 5.6 %collective-permute-start.4 = (bf16[48,128,128]{2,1,0:T(8,128)(2,1)S(1)}, bf16[48,128,128]{2,1,0:T(8,128)(2,1)S(1)}, u32[]{:S(2)}, u32[]{:S(2)}) collective-permute-start(bf16[48,128,128]{2,1,0:T(8,128)(2,1)S(1)} %get-tuple-element.32), channel_id=1, source_target_pairs={{0,1},{1,0},{2,3},{3,2},{4,5},{5,4},{6,7},{7,6},{8,9},{9,8},{10,11... | collective-permute-start | bytes 4718600 | tf_op jit(solution)/shard_map/ppermute | solution.py:393
  73.7 12.9 %collective-permute-start.5 = (bf16[16,128,128]{2,1,0:T(8,128)(2,1)}, bf16[16,128,128]{2,1,0:T(8,128)(2,1)S(1)}, u32[]{:S(2)}, u32[]{:S(2)}) collective-permute-start(bf16[16,128,128]{2,1,0:T(8,128)(2,1)} %get-tuple-element.34), channel_id=1, source_target_pairs={{32,0},{481,1},{64,32},{1,33},{96,64},{33,65},{128,96},{65,97},{16... | collective-permute-start | bytes 1572872 | tf_op jit(solution)/shard_map/ppermute | solution.py:395
  75.7 15.0 %collective-permute-start.6 = (bf16[16,128,128]{2,1,0:T(8,128)(2,1)S(1)}, bf16[16,128,128]{2,1,0:T(8,128)(2,1)S(1)}, u32[]{:S(2)}, u32[]{:S(2)}) collective-permute-start(bf16[16,128,128]{2,1,0:T(8,128)(2,1)S(1)} %get-tuple-element.35), channel_id=1, source_target_pairs={{0,32},{1,481},{32,64},{33,1},{64,96},{65,33},{96,128},{97,65},{12... | collective-permute-start | bytes 1572872 | tf_op jit(solution)/shard_map/ppermute | solution.py:396
  80.2 15.7 %all-to-all-start.2 = ((bf16[16,128,128]{2,1,0:T(8,128)(2,1)}), bf16[16,128,128]{2,1,0:T(8,128)(2,1)S(1)}, u32[]{:S(2)}, u32[]{:S(2)}) async-start(bf16[16,128,128]{2,1,0:T(8,128)(2,1)} %get-tuple-element.28), calls=%async_computation.2 | async-start | bytes 1048576 | tf_op jit(solution)/shard_map/all_to_all | solution.py:377
  95.9 14.6 %all-to-all-start.3 = ((bf16[16,128,128]{2,1,0:T(8,128)(2,1)}), bf16[16,128,128]{2,1,0:T(8,128)(2,1)S(1)}, u32[]{:S(2)}, u32[]{:S(2)}) async-start(bf16[16,128,128]{2,1,0:T(8,128)(2,1)} %finish.1), calls=%async_computation.3 | async-start | bytes 1048576 | tf_op jit(solution)/shard_map/all_to_all | solution.py:377
